TPU v7x, 256 devices: a whole 4x4x8 slice. The times are simulated.
256 devices in a mesh: gx: 16 (over z_lo, y), gy: 16 (over x, z_hi, core).
Axes of the slice: x: 4, y: 4, z: 8 (z_hi: 2, z_lo: 4; z = z_hi * 4 + z_lo), core: 2. Of those that a mesh axis runs over, the one named last changes fastest.
Arguments:
- position: float32 [3, 4194304], P(None, ('gx', 'gy')), may hold values from -3 to 321.2
- velocity: float32 [3, 4194304], P(None, ('gx', 'gy')), may hold values from -0.6 to 0.6
- mass: float32 [4194304], P(('gx', 'gy')), may hold values from 0.01 to 0.04
- smoothing: float32 [4194304], P(('gx', 'gy')), may hold values from 0.8 to 1.25
- energy: float32 [4194304], P(('gx', 'gy')), may hold values from 0.35 to 5.6
- live_blocks: int32 [256], P(('gx', 'gy')), may hold values from 64 to 128, as said below
- send_list: int32 [256, 18, 12], P(('gx', 'gy')), may hold values from 0 to 23, as said below
- nbr_list: int32 [32768, 8], P(('gx', 'gy')), may hold values from 0 to 343, as said below
- nbr_count: int32 [32768], P(('gx', 'gy')), may hold values from 4 to 8
Outputs:
- density: float32 [4194304], P(('gx', 'gy'))
- kick: float32 [3, 4194304], P(None, ('gx', 'gy'))
- heating: float32 [4194304], P(('gx', 'gy'))
Inputs may be any that keep to these rules, and one draw needn't show every extreme that they name: `live_blocks`: the live blocks of a domain are its first ones; some domain has all 128 live and some exactly 64. `send_list`: entries are block indices within the sending domain, all among its first 24 blocks and distinct within one peer list; entry 0 of every list p below 16 is block 0. List p below 16 goes to the domain of fine index p in the same segment, list 16 to the previous segment's domain of the same fine index, list 16 + 1 to the next one's. `nbr_list`: entry 0 of a block's list is the block itself; the others are distinct slots: a live block of the own domain, or a slot 128 + p * 12 + s received from another domain, where p is not the domain's own fine index, p = 16 only if a previous segment exists and p = 17 only if a next one exists.
All inputs are finite; a program needn't handle non-finite values.
Results may differ from a plain program's by a relative error of at most 0.0003.
Values sent between devices are 32-bit elements; how exact they have to be, the bound alone decides.
No kernel may reach another device: no remote copies, remote signals or barrier semaphores. Data moves between devices by JAX's collectives and lax.ppermute only.
A program may use at most 64 MiB of HBM per device.

v0:
```python
import math

import jax
import jax.numpy as jnp
from jax import lax
from jax.sharding import PartitionSpec as P

GAMMA = 5.0 / 3.0
VISC_ALPHA = 1.0
VISC_BETA = 2.0
ETA_SQUARED = 0.01
COURANT = 0.3
KERNEL_NORM = 21.0 / (16.0 * math.pi)
FAR_STEP = 1e30


def padded(array, sides, width):
    for axis, dim in sides:
        size, length = (lax.axis_size(axis), array.shape[dim])
        up = [(i, (i + 1) % size) for i in range(size - 1)]
        down = [(j, i) for i, j in up]
        last = lax.slice_in_dim(array, length - width, length, axis=dim)
        first = lax.slice_in_dim(array, 0, width, axis=dim)
        before = lax.ppermute(last, axis, up)
        after = lax.ppermute(first, axis, down)
        array = jnp.concatenate([before, array, after], axis=dim)
    return array


def kernel_sum(target_pos, target_smooth, source_pos, source_weight):
    squares = sum(
        (
            (target_pos[component][:, None, :] - source_pos[component][:, :, None]) ** 2
            for component in range(3)
        )
    )
    ratio = jnp.sqrt(squares) / target_smooth[:, None, :]
    taper = jnp.maximum(1.0 - 0.5 * ratio, 0.0)
    profile = taper**4 * (1.0 + 2.0 * ratio)
    total = jnp.sum(source_weight[:, :, None] * profile, axis=1)
    return KERNEL_NORM / target_smooth**3 * total


def pressure_terms(dens, thermal):
    return ((GAMMA - 1.0) * thermal / dens, jnp.sqrt(GAMMA * (GAMMA - 1.0) * thermal))


def force_sum(target, source, source_weight, source_valid):
    target_pos, target_vel, target_smooth, target_dens, target_press, target_sound = target
    source_pos, source_vel, source_smooth, source_dens, source_press, source_sound = source
    offsets = [
        target_pos[component][:, None, :] - source_pos[component][:, :, None]
        for component in range(3)
    ]
    moving = [
        target_vel[component][:, None, :] - source_vel[component][:, :, None]
        for component in range(3)
    ]
    squares = offsets[0] * offsets[0] + offsets[1] * offsets[1] + offsets[2] * offsets[2]
    closing = offsets[0] * moving[0] + offsets[1] * moving[1] + offsets[2] * moving[2]
    mean_smooth = 0.5 * (target_smooth[:, None, :] + source_smooth[:, :, None])
    taper = jnp.maximum(1.0 - 0.5 * jnp.sqrt(squares) / mean_smooth, 0.0)
    slope = -5.0 * KERNEL_NORM * taper**3 / mean_smooth**5
    approach = (
        mean_smooth
        * jnp.minimum(closing, 0.0)
        / (squares + ETA_SQUARED * mean_smooth * mean_smooth)
    )
    mean_sound = 0.5 * (target_sound[:, None, :] + source_sound[:, :, None])
    mean_dens = 0.5 * (target_dens[:, None, :] + source_dens[:, :, None])
    visc = (-VISC_ALPHA * mean_sound * approach + VISC_BETA * approach * approach) / mean_dens
    coef = (
        source_weight[:, :, None]
        * (target_press[:, None, :] + source_press[:, :, None] + visc)
        * slope
    )
    accel = jnp.stack([-jnp.sum(coef * offset, axis=1) for offset in offsets])
    rate = 0.5 * jnp.sum(coef * closing, axis=1)
    signal = jnp.max(jnp.where(source_valid[:, :, None], -approach, 0.0), axis=1)
    return (accel, rate, signal)


def shards(
    position, velocity, mass, smoothing, energy, live_blocks, send_list, nbr_list, nbr_count
):
    peer_count = lax.axis_size("gy")
    block_count = nbr_count.shape[0]
    block_size = mass.shape[0] // block_count
    slot_count = send_list.shape[2]
    list_width = nbr_list.shape[1]
    places = position.reshape(3, block_count, block_size)
    speeds = velocity.reshape(3, block_count, block_size)
    masses = mass.reshape(block_count, block_size)
    smooth = smoothing.reshape(block_count, block_size)
    thermal = energy.reshape(block_count, block_size)
    to_fine = send_list[0, :peer_count].reshape(-1)
    to_segment = send_list[0, peer_count:].reshape(-1)
    stack = jnp.concatenate([places, speeds, masses[None], smooth[None], thermal[None]], axis=0)
    height = stack.shape[0]
    outgoing = stack[:, to_fine].reshape(height, peer_count, slot_count, block_size)
    arrived = lax.all_to_all(outgoing, "gy", split_axis=1, concat_axis=1, tiled=True)
    border = padded(stack[:, to_segment], (("gx", 1),), slot_count)
    first = jnp.concatenate(
        [
            arrived.reshape(height, peer_count * slot_count, block_size),
            border[:, :slot_count],
            border[:, 3 * slot_count :],
        ],
        axis=1,
    )
    ghost_pos = first[0:3]
    ghost_vel = first[3:6]
    ghost_mass = first[6]
    ghost_smooth = first[7]
    ghost_thermal = first[8]
    wide_pos = jnp.concatenate([places, ghost_pos], axis=1)
    wide_mass = jnp.concatenate([masses, ghost_mass], axis=0)
    group = min(block_count, 8)
    turns = block_count // group
    usable = jnp.arange(list_width, dtype=jnp.int32)[None, :] < nbr_count[:, None]
    usable_rows = jnp.repeat(usable, block_size, axis=1).reshape(
        turns, group, list_width * block_size
    )
    grouped_lists = nbr_list.reshape(turns, group, list_width)

    def density_group(inputs):
        chosen, allowed, target_pos, target_smooth = inputs
        source_pos = wide_pos[:, chosen].reshape(3, group, list_width * block_size)
        weight = jnp.where(allowed, wide_mass[chosen].reshape(group, list_width * block_size), 0.0)
        return kernel_sum(target_pos, target_smooth, source_pos, weight)

    grouped_pos = jnp.moveaxis(places.reshape(3, turns, group, block_size), 1, 0)
    rho = lax.map(
        density_group,
        (grouped_lists, usable_rows, grouped_pos, smooth.reshape(turns, group, block_size)),
    )
    rho = rho.reshape(block_count, block_size)
    press, sound = pressure_terms(rho, thermal)
    stack = rho[None]
    height = stack.shape[0]
    outgoing = stack[:, to_fine].reshape(height, peer_count, slot_count, block_size)
    arrived = lax.all_to_all(outgoing, "gy", split_axis=1, concat_axis=1, tiled=True)
    border = padded(stack[:, to_segment], (("gx", 1),), slot_count)
    second = jnp.concatenate(
        [
            arrived.reshape(height, peer_count * slot_count, block_size),
            border[:, :slot_count],
            border[:, 3 * slot_count :],
        ],
        axis=1,
    )
    ghost_rho = second[0]
    ghost_press, ghost_sound = pressure_terms(ghost_rho, ghost_thermal)
    own_table = jnp.concatenate(
        [places, speeds, masses[None], smooth[None], rho[None], press[None], sound[None]], axis=0
    )
    ghost_table = jnp.concatenate(
        [
            ghost_pos,
            ghost_vel,
            ghost_mass[None],
            ghost_smooth[None],
            ghost_rho[None],
            ghost_press[None],
            ghost_sound[None],
        ],
        axis=0,
    )
    wide_table = jnp.concatenate([own_table, ghost_table], axis=1)
    row_count = own_table.shape[0]

    def force_group(inputs):
        chosen, allowed, target_rows = inputs
        source_rows = wide_table[:, chosen].reshape(row_count, group, list_width * block_size)
        weight = jnp.where(allowed, source_rows[6], 0.0)
        target = (
            target_rows[0:3],
            target_rows[3:6],
            target_rows[7],
            target_rows[8],
            target_rows[9],
            target_rows[10],
        )
        source = (
            source_rows[0:3],
            source_rows[3:6],
            source_rows[7],
            source_rows[8],
            source_rows[9],
            source_rows[10],
        )
        return force_sum(target, source, weight, allowed)

    grouped_rows = jnp.moveaxis(own_table.reshape(row_count, turns, group, block_size), 1, 0)
    accel, rate, signal = lax.map(force_group, (grouped_lists, usable_rows, grouped_rows))
    accel = jnp.moveaxis(accel, 1, 0).reshape(3, block_count, block_size)
    rate = rate.reshape(block_count, block_size)
    signal = signal.reshape(block_count, block_size)
    alive = jnp.arange(block_count, dtype=jnp.int32)[:, None] < live_blocks[0]
    alive = jnp.broadcast_to(alive, (block_count, block_size))
    step = COURANT * smooth / (sound + 1.2 * (VISC_ALPHA * sound + VISC_BETA * signal))
    local_least = jnp.min(jnp.where(alive, step, FAR_STEP))
    timestep = lax.pmin(local_least, ("gx", "gy"))
    density = jnp.where(alive, rho, 0.0).reshape(-1)
    kick = jnp.where(alive[None], timestep * accel, 0.0).reshape(3, -1)
    heating = jnp.where(alive, timestep * rate, 0.0).reshape(-1)
    return (density, kick, heating)


def solution(mesh):
    return jax.shard_map(
        shards,
        mesh=mesh,
        in_specs=(
            P(None, ("gx", "gy")),
            P(None, ("gx", "gy")),
            P(("gx", "gy")),
            P(("gx", "gy")),
            P(("gx", "gy")),
            P(("gx", "gy")),
            P(("gx", "gy"), None, None),
            P(("gx", "gy"), None),
            P(("gx", "gy")),
        ),
        out_specs=(P(("gx", "gy")), P(None, ("gx", "gy")), P(("gx", "gy"))),
        check_vma=False,
    )
```

profile of v0, /device:TPU:1, one launch (start us, length us, event | category | flops | bytes accessed | tf_op | source)
XLA Modules:
  0.0 610.9 jit_solution(18320119831589012151)
XLA Ops:
  9.6 12.6 %all-to-all-start = ((f32[9,16,12,128]{3,2,0,1:T(8,128)}), f32[9,16,12,128]{3,2,0,1:T(8,128)S(1)}, u32[]{:S(2)}, u32[]{:S(2)}) async-start(f32[9,16,12,128]{3,2,0,1:T(8,128)} %copy.49), calls=%async_computation | async-start | bytes 2359296 | tf_op jit(solution)/shard_map/all_to_all | solution.py:101
  31.6 15.0 %all-to-all-done = f32[9,16,12,128]{3,2,0,1:T(8,128)S(1)} async-done(((f32[9,16,12,128]{3,2,0,1:T(8,128)}), f32[9,16,12,128]{3,2,0,1:T(8,128)S(1)}, u32[]{:S(2)}, u32[]{:S(2)}) %all-to-all-start) | async-done | bytes 884768 | tf_op jit(solution)/shard_map/all_to_all | solution.py:101
  47.2 140.5 %while.26 = (s32[]{:T(128)}, f32[16,8,128]{2,1,0:T(8,128)S(1)}, f32[16,8,128]{2,1,0:T(8,128)S(1)}, pred[16,8,1024]{2,1,0:T(8,128)(4,1)}, s32[16,8,8]{2,1,0:T(8,1...) while((s32[]{:T(128)}, f32[16,8,128]{2,1,0:T(8,128)S(1)}, ...), condition=%wide.region_2.3_spmd, body=%wide.region_0.2_spmd.sunk | while | flops 19935424 | bytes 1021817 | solution.py:133
  68.6 4.9 multiply_reduce_fusion.4
  77.4 4.9 multiply_reduce_fusion.4
  86.2 4.9 multiply_reduce_fusion.4
  103.8 4.9 multiply_reduce_fusion.4
  112.5 4.9 multiply_reduce_fusion.4
  121.3 4.9 multiply_reduce_fusion.4
  138.9 4.9 multiply_reduce_fusion.4
  147.7 4.9 multiply_reduce_fusion.4
  156.4 4.9 multiply_reduce_fusion.4
  174.0 4.9 multiply_reduce_fusion.4
  194.9 9.8 %all-to-all-start.1 = ((f32[1,16,12,128]{3,0,2,1:T(1,128)}), f32[1,16,12,128]{3,0,2,1:T(1,128)}, u32[]{:S(2)}, u32[]{:S(2)}) async-start(f32[1,16,12,128]{3,0,2,1:T(1,128)} %bitcast.51), calls=%async_computation.1 | async-start | bytes 196608 | tf_op jit(solution)/shard_map/all_to_all | solution.py:142
  218.6 303.8 %while.27 = (s32[]{:T(128)}, f32[16,3,8,128]{3,2,1,0:T(8,128)}, f32[16,8,128]{2,1,0:T(8,128)}, f32[16,8,128]{2,1,0:T(8,128)}, pred[16,8,1024]{2,1,0:T(8,128)(4,1...) while((s32[]{:T(128)}, f32[16,3,8,128]{3,2,1,0:T(8,128)}, ...), condition=%wide.region_9.10_spmd, body=%wide.region_3.9_spmd.sunk | while | flops 60831936 | bytes 2852473 | solution.py:195
  222.6 13.7 %multiply_reduce_fusion.5 = (f32[8,128]{1,0:T(8,128)S(1)}, f32[8,128]{1,0:T(8,128)S(1)}, f32[8,128]{1,0:T(8,128)S(1)}, f32[8,128]{1,0:T(8,128)S(1)}, f32[8,128]{1,0:T(8,128)S(1)}) fusion(f32[8,1024]{1,0:T(8,128)S(1)} %bitcast.325, f32[8,128]{1,0:T(8,128)S(1)} %get-tuple-element.432, f32[8,1024]{1,0:T(8,128)S(1)} %bitcast.326, ...), kind=kLoop, calls=%fused_computation.65.clone.1 | loop fusion | flops 60812288 | bytes 430080 | tf_op jit(solution)/shard_map/while/body/eval_jaxpr/reduce_sum | solution.py:78
  241.6 13.7 %multiply_reduce_fusion.5 = (f32[8,128]{1,0:T(8,128)S(1)}, f32[8,128]{1,0:T(8,128)S(1)}, f32[8,128]{1,0:T(8,128)S(1)}, f32[8,128]{1,0:T(8,128)S(1)}, f32[8,128]{1,0:T(8,128)S(1)}) fusion(f32[8,1024]{1,0:T(8,128)S(1)} %bitcast.325, f32[8,128]{1,0:T(8,128)S(1)} %get-tuple-element.432, f32[8,1024]{1,0:T(8,128)S(1)} %bitcast.326, ...), kind=kLoop, calls=%fused_computation.65.clone.1 | loop fusion | flops 60812288 | bytes 430080 | tf_op jit(solution)/shard_map/while/body/eval_jaxpr/reduce_sum | solution.py:78
  260.6 13.7 %multiply_reduce_fusion.5 = (f32[8,128]{1,0:T(8,128)S(1)}, f32[8,128]{1,0:T(8,128)S(1)}, f32[8,128]{1,0:T(8,128)S(1)}, f32[8,128]{1,0:T(8,128)S(1)}, f32[8,128]{1,0:T(8,128)S(1)}) fusion(f32[8,1024]{1,0:T(8,128)S(1)} %bitcast.325, f32[8,128]{1,0:T(8,128)S(1)} %get-tuple-element.432, f32[8,1024]{1,0:T(8,128)S(1)} %bitcast.326, ...), kind=kLoop, calls=%fused_computation.65.clone.1 | loop fusion | flops 60812288 | bytes 430080 | tf_op jit(solution)/shard_map/while/body/eval_jaxpr/reduce_sum | solution.py:78
  279.6 13.7 %multiply_reduce_fusion.5 = (f32[8,128]{1,0:T(8,128)S(1)}, f32[8,128]{1,0:T(8,128)S(1)}, f32[8,128]{1,0:T(8,128)S(1)}, f32[8,128]{1,0:T(8,128)S(1)}, f32[8,128]{1,0:T(8,128)S(1)}) fusion(f32[8,1024]{1,0:T(8,128)S(1)} %bitcast.325, f32[8,128]{1,0:T(8,128)S(1)} %get-tuple-element.432, f32[8,1024]{1,0:T(8,128)S(1)} %bitcast.326, ...), kind=kLoop, calls=%fused_computation.65.clone.1 | loop fusion | flops 60812288 | bytes 430080 | tf_op jit(solution)/shard_map/while/body/eval_jaxpr/reduce_sum | solution.py:78
  298.6 13.7 %multiply_reduce_fusion.5 = (f32[8,128]{1,0:T(8,128)S(1)}, f32[8,128]{1,0:T(8,128)S(1)}, f32[8,128]{1,0:T(8,128)S(1)}, f32[8,128]{1,0:T(8,128)S(1)}, f32[8,128]{1,0:T(8,128)S(1)}) fusion(f32[8,1024]{1,0:T(8,128)S(1)} %bitcast.325, f32[8,128]{1,0:T(8,128)S(1)} %get-tuple-element.432, f32[8,1024]{1,0:T(8,128)S(1)} %bitcast.326, ...), kind=kLoop, calls=%fused_computation.65.clone.1 | loop fusion | flops 60812288 | bytes 430080 | tf_op jit(solution)/shard_map/while/body/eval_jaxpr/reduce_sum | solution.py:78
  317.6 13.7 %multiply_reduce_fusion.5 = (f32[8,128]{1,0:T(8,128)S(1)}, f32[8,128]{1,0:T(8,128)S(1)}, f32[8,128]{1,0:T(8,128)S(1)}, f32[8,128]{1,0:T(8,128)S(1)}, f32[8,128]{1,0:T(8,128)S(1)}) fusion(f32[8,1024]{1,0:T(8,128)S(1)} %bitcast.325, f32[8,128]{1,0:T(8,128)S(1)} %get-tuple-element.432, f32[8,1024]{1,0:T(8,128)S(1)} %bitcast.326, ...), kind=kLoop, calls=%fused_computation.65.clone.1 | loop fusion | flops 60812288 | bytes 430080 | tf_op jit(solution)/shard_map/while/body/eval_jaxpr/reduce_sum | solution.py:78
  336.5 13.7 %multiply_reduce_fusion.5 = (f32[8,128]{1,0:T(8,128)S(1)}, f32[8,128]{1,0:T(8,128)S(1)}, f32[8,128]{1,0:T(8,128)S(1)}, f32[8,128]{1,0:T(8,128)S(1)}, f32[8,128]{1,0:T(8,128)S(1)}) fusion(f32[8,1024]{1,0:T(8,128)S(1)} %bitcast.325, f32[8,128]{1,0:T(8,128)S(1)} %get-tuple-element.432, f32[8,1024]{1,0:T(8,128)S(1)} %bitcast.326, ...), kind=kLoop, calls=%fused_computation.65.clone.1 | loop fusion | flops 60812288 | bytes 430080 | tf_op jit(solution)/shard_map/while/body/eval_jaxpr/reduce_sum | solution.py:78
  355.5 13.7 %multiply_reduce_fusion.5 = (f32[8,128]{1,0:T(8,128)S(1)}, f32[8,128]{1,0:T(8,128)S(1)}, f32[8,128]{1,0:T(8,128)S(1)}, f32[8,128]{1,0:T(8,128)S(1)}, f32[8,128]{1,0:T(8,128)S(1)}) fusion(f32[8,1024]{1,0:T(8,128)S(1)} %bitcast.325, f32[8,128]{1,0:T(8,128)S(1)} %get-tuple-element.432, f32[8,1024]{1,0:T(8,128)S(1)} %bitcast.326, ...), kind=kLoop, calls=%fused_computation.65.clone.1 | loop fusion | flops 60812288 | bytes 430080 | tf_op jit(solution)/shard_map/while/body/eval_jaxpr/reduce_sum | solution.py:78
  374.5 13.7 %multiply_reduce_fusion.5 = (f32[8,128]{1,0:T(8,128)S(1)}, f32[8,128]{1,0:T(8,128)S(1)}, f32[8,128]{1,0:T(8,128)S(1)}, f32[8,128]{1,0:T(8,128)S(1)}, f32[8,128]{1,0:T(8,128)S(1)}) fusion(f32[8,1024]{1,0:T(8,128)S(1)} %bitcast.325, f32[8,128]{1,0:T(8,128)S(1)} %get-tuple-element.432, f32[8,1024]{1,0:T(8,128)S(1)} %bitcast.326, ...), kind=kLoop, calls=%fused_computation.65.clone.1 | loop fusion | flops 60812288 | bytes 430080 | tf_op jit(solution)/shard_map/while/body/eval_jaxpr/reduce_sum | solution.py:78
  393.5 13.7 %multiply_reduce_fusion.5 = (f32[8,128]{1,0:T(8,128)S(1)}, f32[8,128]{1,0:T(8,128)S(1)}, f32[8,128]{1,0:T(8,128)S(1)}, f32[8,128]{1,0:T(8,128)S(1)}, f32[8,128]{1,0:T(8,128)S(1)}) fusion(f32[8,1024]{1,0:T(8,128)S(1)} %bitcast.325, f32[8,128]{1,0:T(8,128)S(1)} %get-tuple-element.432, f32[8,1024]{1,0:T(8,128)S(1)} %bitcast.326, ...), kind=kLoop, calls=%fused_computation.65.clone.1 | loop fusion | flops 60812288 | bytes 430080 | tf_op jit(solution)/shard_map/while/body/eval_jaxpr/reduce_sum | solution.py:78
  412.5 13.7 %multiply_reduce_fusion.5 = (f32[8,128]{1,0:T(8,128)S(1)}, f32[8,128]{1,0:T(8,128)S(1)}, f32[8,128]{1,0:T(8,128)S(1)}, f32[8,128]{1,0:T(8,128)S(1)}, f32[8,128]{1,0:T(8,128)S(1)}) fusion(f32[8,1024]{1,0:T(8,128)S(1)} %bitcast.325, f32[8,128]{1,0:T(8,128)S(1)} %get-tuple-element.432, f32[8,1024]{1,0:T(8,128)S(1)} %bitcast.326, ...), kind=kLoop, calls=%fused_computation.65.clone.1 | loop fusion | flops 60812288 | bytes 430080 | tf_op jit(solution)/shard_map/while/body/eval_jaxpr/reduce_sum | solution.py:78
  431.5 13.7 %multiply_reduce_fusion.5 = (f32[8,128]{1,0:T(8,128)S(1)}, f32[8,128]{1,0:T(8,128)S(1)}, f32[8,128]{1,0:T(8,128)S(1)}, f32[8,128]{1,0:T(8,128)S(1)}, f32[8,128]{1,0:T(8,128)S(1)}) fusion(f32[8,1024]{1,0:T(8,128)S(1)} %bitcast.325, f32[8,128]{1,0:T(8,128)S(1)} %get-tuple-element.432, f32[8,1024]{1,0:T(8,128)S(1)} %bitcast.326, ...), kind=kLoop, calls=%fused_computation.65.clone.1 | loop fusion | flops 60812288 | bytes 430080 | tf_op jit(solution)/shard_map/while/body/eval_jaxpr/reduce_sum | solution.py:78
  450.5 13.7 %multiply_reduce_fusion.5 = (f32[8,128]{1,0:T(8,128)S(1)}, f32[8,128]{1,0:T(8,128)S(1)}, f32[8,128]{1,0:T(8,128)S(1)}, f32[8,128]{1,0:T(8,128)S(1)}, f32[8,128]{1,0:T(8,128)S(1)}) fusion(f32[8,1024]{1,0:T(8,128)S(1)} %bitcast.325, f32[8,128]{1,0:T(8,128)S(1)} %get-tuple-element.432, f32[8,1024]{1,0:T(8,128)S(1)} %bitcast.326, ...), kind=kLoop, calls=%fused_computation.65.clone.1 | loop fusion | flops 60812288 | bytes 430080 | tf_op jit(solution)/shard_map/while/body/eval_jaxpr/reduce_sum | solution.py:78
  469.4 13.7 %multiply_reduce_fusion.5 = (f32[8,128]{1,0:T(8,128)S(1)}, f32[8,128]{1,0:T(8,128)S(1)}, f32[8,128]{1,0:T(8,128)S(1)}, f32[8,128]{1,0:T(8,128)S(1)}, f32[8,128]{1,0:T(8,128)S(1)}) fusion(f32[8,1024]{1,0:T(8,128)S(1)} %bitcast.325, f32[8,128]{1,0:T(8,128)S(1)} %get-tuple-element.432, f32[8,1024]{1,0:T(8,128)S(1)} %bitcast.326, ...), kind=kLoop, calls=%fused_computation.65.clone.1 | loop fusion | flops 60812288 | bytes 430080 | tf_op jit(solution)/shard_map/while/body/eval_jaxpr/reduce_sum | solution.py:78
  488.4 13.7 %multiply_reduce_fusion.5 = (f32[8,128]{1,0:T(8,128)S(1)}, f32[8,128]{1,0:T(8,128)S(1)}, f32[8,128]{1,0:T(8,128)S(1)}, f32[8,128]{1,0:T(8,128)S(1)}, f32[8,128]{1,0:T(8,128)S(1)}) fusion(f32[8,1024]{1,0:T(8,128)S(1)} %bitcast.325, f32[8,128]{1,0:T(8,128)S(1)} %get-tuple-element.432, f32[8,1024]{1,0:T(8,128)S(1)} %bitcast.326, ...), kind=kLoop, calls=%fused_computation.65.clone.1 | loop fusion | flops 60812288 | bytes 430080 | tf_op jit(solution)/shard_map/while/body/eval_jaxpr/reduce_sum | solution.py:78
  507.4 13.7 %multiply_reduce_fusion.5 = (f32[8,128]{1,0:T(8,128)S(1)}, f32[8,128]{1,0:T(8,128)S(1)}, f32[8,128]{1,0:T(8,128)S(1)}, f32[8,128]{1,0:T(8,128)S(1)}, f32[8,128]{1,0:T(8,128)S(1)}) fusion(f32[8,1024]{1,0:T(8,128)S(1)} %bitcast.325, f32[8,128]{1,0:T(8,128)S(1)} %get-tuple-element.432, f32[8,1024]{1,0:T(8,128)S(1)} %bitcast.326, ...), kind=kLoop, calls=%fused_computation.65.clone.1 | loop fusion | flops 60812288 | bytes 430080 | tf_op jit(solution)/shard_map/while/body/eval_jaxpr/reduce_sum | solution.py:78
  524.0 82.1 %pmin.7 = f32[]{:T(128)} all-reduce(f32[]{:T(128)} %fusion.28), channel_id=1, replica_groups=mesh['gx'=16,'gy'=16] {'gx','gy'}, use_global_device_ids=true, to_apply=%region_11.12 | all-reduce | flops 1 | bytes 8 | tf_op jit(solution)/shard_map/pmin | solution.py:203
  (673 shorter events, 218.3 us)
Async XLA Ops:
  6.8 21.9 %copy-start.11 = (s32[128]{0:T(128)S(1)}, s32[128]{0:T(128)}, u32[]{:S(2)}) copy-start(s32[128]{0:T(128)} %param.21) | copy-start | bytes 1540
  6.8 22.0 %copy-start = (f32[3,16384]{1,0:T(4,128)S(1)}, f32[3,16384]{1,0:T(4,128)}, u32[]{:S(2)}) copy-start(f32[3,16384]{1,0:T(4,128)} %param.13) | copy-start | bytes 589828
  6.8 22.1 %copy-start.2 = (f32[3,16384]{1,0:T(4,128)S(1)}, f32[3,16384]{1,0:T(4,128)}, u32[]{:S(2)}) copy-start(f32[3,16384]{1,0:T(4,128)} %param.14) | copy-start | bytes 589828
  6.8 22.1 %copy-start.8 = (f32[16384]{0:T(1024)S(1)}, f32[16384]{0:T(1024)}, u32[]{:S(2)}) copy-start(f32[16384]{0:T(1024)} %param.15) | copy-start | bytes 196612
  6.8 22.1 %copy-start.5 = (f32[16384]{0:T(1024)S(1)}, f32[16384]{0:T(1024)}, u32[]{:S(2)}) copy-start(f32[16384]{0:T(1024)} %param.16) | copy-start | bytes 196612
  9.6 21.1 %copy-start.10 = (s32[128,8]{0,1:T(8,128)S(1)}, s32[128,8]{0,1:T(8,128)}, u32[]{:S(2)}) copy-start(s32[128,8]{0,1:T(8,128)} %param.20) | copy-start | bytes 12292
  9.6 37.0 %all-to-all-start = ((f32[9,16,12,128]{3,2,0,1:T(8,128)}), f32[9,16,12,128]{3,2,0,1:T(8,128)S(1)}, u32[]{:S(2)}, u32[]{:S(2)}) async-start(f32[9,16,12,128]{3,2,0,1:T(8,128)} %copy.49), calls=%async_computation | async-start | bytes 2359296 | tf_op jit(solution)/shard_map/all_to_all | solution.py:101
  22.8 8.7 %collective-permute-start.1 = (f32[9,12,128]{2,0,1:T(8,128)S(1)}, f32[9,12,128]{2,0,1:T(8,128)S(1)}, u32[]{:S(2)}, u32[]{:S(2)}) collective-permute-start(f32[9,12,128]{2,0,1:T(8,128)S(1)} %get-tuple-element.276), channel_id=1, source_target_pairs={{16,0},{32,16},{48,32},{64,48},{80,64},{96,80},{112,96},{128,112},... | collective-permute-start | bytes 165896 | tf_op jit(solution)/shard_map/ppermute | solution.py:25
  24.1 7.4 %collective-permute-start = (f32[9,12,128]{2,0,1:T(8,128)S(1)}, f32[9,12,128]{2,0,1:T(8,128)S(1)}, u32[]{:S(2)}, u32[]{:S(2)}) collective-permute-start(f32[9,12,128]{2,0,1:T(8,128)S(1)} %get-tuple-element.275), channel_id=1, source_target_pairs={{0,16},{16,32},{32,48},{48,64},{64,80},{80,96},{96,112},{112,128},... | collective-permute-start | bytes 165896 | tf_op jit(solution)/shard_map/ppermute | solution.py:24
  28.9 2.6 copy-start.9
  31.5 15.3 %copy-start.6 = (f32[9,12,128]{2,1,0:T(8,128)}, f32[9,12,128]{2,1,0:T(8,128)S(1)}, u32[]{:S(2)}) copy-start(f32[9,12,128]{2,1,0:T(8,128)S(1)} %copy.53) | copy-start | bytes 165892
  31.6 15.3 %copy-start.7 = (f32[9,12,128]{2,1,0:T(8,128)}, f32[9,12,128]{2,1,0:T(8,128)S(1)}, u32[]{:S(2)}) copy-start(f32[9,12,128]{2,1,0:T(8,128)S(1)} %copy.52) | copy-start | bytes 165892
  46.9 160.6 %copy-start.1 = (f32[9,216,128]{2,1,0:T(8,128)}, f32[9,216,128]{2,1,0:T(8,128)S(1)}, u32[]{:S(2)}) copy-start(f32[9,216,128]{2,1,0:T(8,128)S(1)} %pad_maximum_fusion) | copy-start | bytes 2985988
  47.2 157.5 %copy-start.4 = (f32[16384]{0:T(1024)S(1)}, f32[16384]{0:T(1024)}, u32[]{:S(2)}) copy-start(f32[16384]{0:T(1024)} %param.17) | copy-start | bytes 196612
  187.8 19.7 %copy-start.3 = (f32[3,16384]{1,0:T(4,128)S(1)}, f32[3,16384]{1,0:T(4,128)}, u32[]{:S(2)}) copy-start(f32[3,16384]{1,0:T(4,128)} %param.14) | copy-start | bytes 589828
  189.7 21.3 %collective-permute-start.3 = (f32[1,12,128]{2,1,0:T(8,128)S(1)}, f32[1,12,128]{2,1,0:T(8,128)S(1)}, u32[]{:S(2)}, u32[]{:S(2)}) collective-permute-start(f32[1,12,128]{2,1,0:T(8,128)S(1)} %get-tuple-element.280), channel_id=1, source_target_pairs={{16,0},{32,16},{48,32},{64,48},{80,64},{96,80},{112,96},{128,112},... | collective-permute-start | bytes 18440 | tf_op jit(solution)/shard_map/ppermute | solution.py:25
  190.9 20.0 %collective-permute-start.2 = (f32[1,12,128]{2,1,0:T(8,128)S(1)}, f32[1,12,128]{2,1,0:T(8,128)S(1)}, u32[]{:S(2)}, u32[]{:S(2)}) collective-permute-start(f32[1,12,128]{2,1,0:T(8,128)S(1)} %get-tuple-element.279), channel_id=1, source_target_pairs={{0,16},{16,32},{32,48},{48,64},{64,80},{80,96},{96,112},{112,128},... | collective-permute-start | bytes 18440 | tf_op jit(solution)/shard_map/ppermute | solution.py:24
  194.9 19.6 %all-to-all-start.1 = ((f32[1,16,12,128]{3,0,2,1:T(1,128)}), f32[1,16,12,128]{3,0,2,1:T(1,128)}, u32[]{:S(2)}, u32[]{:S(2)}) async-start(f32[1,16,12,128]{3,0,2,1:T(1,128)} %bitcast.51), calls=%async_computation.1 | async-start | bytes 196608 | tf_op jit(solution)/shard_map/all_to_all | solution.py:142
  207.5 8.0 %slice-start = ((f32[9,216,128]{2,1,0:T(8,128)}), f32[8,216,128]{2,1,0:T(8,128)S(1)}, s32[]{:S(2)}) async-start(f32[9,216,128]{2,1,0:T(8,128)} %copy-done.1), calls=%async_computation.2 | async-start | bytes 1769472 | tf_op jit(solution)/shard_map/slice | solution.py:111
where the time goes:
time: 616 us; the launch traced here: 611 us
  other arithmetic  374 us (61%)
  local copies, waits for them, and re-layouts  98.6 us (16%)
  blocking collectives  82.1 us (13%)
  starting transfers between devices  32.9 us (5%)
  waiting for transfers between devices  18.6 us (3%)
    reduce_sum x16, other arithmetic, force_sum(): rate = 0.5 * jnp.sum(coef * closing, axis=1)  219 us
    pmin x1, blocking collectives, shards(): timestep = lax.pmin(local_least, ('gx', 'gy'))  82.1 us
    reduce_sum x16, other arithmetic, kernel_sum(): total = jnp.sum(source_weight[:, :, None] * profile, axis=1)  79 us
    all_to_all x2, starting transfers between devices, shards(): lax.all_to_all(outgoing, 'gy', split_axis=1, concat_axis=1, tiled=True)  22.3 us
    all_to_all x2, waiting for transfers between devices, shards(): lax.all_to_all(outgoing, 'gy', split_axis=1, concat_axis=1, tiled=True)  18.6 us
    slice x16, local copies, waits for them, and re-layouts, force_group(): weight = jnp.where(allowed, source_rows[6], 0.0)  15 us
    dynamic_slice x16, local copies, waits for them, and re-layouts, shards(): lax.map(force_group, (grouped_lists, usable_rows, grouped_rows))  12.8 us
  transfers between devices with their start and end apart: 6, of which 2 were waited for; matrix products, arithmetic and copies ran while one was open for 2% of the time, Pallas kernels for 0%

commit v1 on v0

v1 whole, which is shorter than its diff:
```python
import math

import jax
import jax.numpy as jnp
from jax import lax
from jax.experimental import pallas as pl
from jax.experimental.pallas import tpu as pltpu
from jax.sharding import PartitionSpec as P

COURANT = 0.3
FAR_STEP = 1e30
TINY = 1e-30
LANES = 128
CHUNK = 8
FIRST = 24
PEER_TILES = 14
PEER_ROWS = 16
F32 = jnp.float32

SMEM = pl.BlockSpec(memory_space=pltpu.SMEM)
VMEM = pl.BlockSpec(memory_space=pltpu.VMEM)


def struct(*shape):
    return jax.ShapeDtypeStruct(shape, F32)


def columns(row):
    return jnp.broadcast_to(row, (LANES, LANES)).T


def spread(row):
    return jnp.broadcast_to(row, (CHUNK, LANES))


def pack_kernel(send, position, velocity, mass, smooth, energy, table, fine, lower, upper):
    blocks = mass.shape[0]

    def build(k, carry):
        at = pl.ds(pl.multiple_of(k * LANES, LANES), LANES)
        row = pl.ds(k, 1)
        table[k] = jnp.concatenate(
            [position[:, at], mass[row, :], -2.0 * velocity[:, at], smooth[row, :]], axis=0
        )
        return carry

    lax.fori_loop(0, blocks, build, 0)

    def fill(target, first_tile, p):
        for s in range(12):
            k = send[p * 12 + s]
            target[first_tile + s] = table[k]
            target[first_tile + 12 + s // 8, s % 8 : s % 8 + 1, :] = energy[pl.ds(k, 1), :]
        target[first_tile + 13, 4:8, :] = jnp.zeros((4, LANES), F32)

    def peer(p, carry):
        fill(fine, p * PEER_TILES, p)
        return carry

    lax.fori_loop(0, 16, peer, 0)
    fill(lower, 0, 16)
    fill(upper, 0, 17)


def density_sum(cols, rows_of, count):
    def one(j, sums):
        xs, ys, zs, ms = rows_of(j)
        out = []
        for c in range(LANES // CHUNK):
            at = pl.ds(c * CHUNK, CHUNK)
            dx = cols[0, at, :] - xs
            dy = cols[1, at, :] - ys
            dz = cols[2, at, :] - zs
            r2 = dx * dx + dy * dy + dz * dz
            u2 = r2 * cols[3, at, :]
            u = u2 * lax.rsqrt(jnp.maximum(u2, TINY))
            t = jnp.maximum(1.0 - u, 0.0)
            t2 = t * t
            out.append(sums[c] + (t2 * ms) * (t2 * (1.25 - t)))
        return tuple(out)

    zero = tuple(jnp.zeros((CHUNK, LANES), F32) for _ in range(LANES // CHUNK))
    sums = lax.fori_loop(0, count, one, zero)
    return jnp.sum(jnp.concatenate(sums, axis=0).T, axis=0, keepdims=True)


def density_columns(cols, table, t):
    for f in range(3):
        cols[f] = columns(table[t, f : f + 1, :])
    h = table[t, 7:8, :]
    cols[3] = columns(0.25 / (h * h))
    return (21.0 / (4.0 * math.pi)) / (h * h * h)


def density_rows(source, tile):
    return [spread(source[tile, f : f + 1, :]) for f in range(4)]


def local_density_kernel(lists, counts, live, table, out, cols):
    out[...] = jnp.zeros_like(out)

    def block(t, carry):
        norm = density_columns(cols, table, t)
        total = density_sum(cols, lambda j: density_rows(table, lists[t * 8 + j]), counts[t])
        out[pl.ds(t, 1), :] = norm * total
        return carry

    lax.fori_loop(0, live[0], block, 0)


def ghost_density(lists, counts, table, ghosts, out, cols, lo, hi):
    def block(t, carry):
        @pl.when(counts[t] > 0)
        def _():
            norm = density_columns(cols, table, t)

            def rows_of(j):
                g = lists[t * 8 + j]
                return density_rows(ghosts, g - 2 * (g // PEER_ROWS))

            total = density_sum(cols, rows_of, counts[t])
            out[pl.ds(t, 1), :] += norm * total

        return carry

    lax.fori_loop(lo, hi, block, 0)


def first_density_kernel(send, lists, counts, table, ghosts, rho, first, fine, lower, upper, cols):
    first[...] = rho[0:FIRST, :]
    ghost_density(lists, counts, table, ghosts, first, cols, 0, FIRST)

    def fill(target, first_row, p):
        for s in range(12):
            target[pl.ds(first_row + s, 1), :] = first[pl.ds(send[p * 12 + s], 1), :]
        for s in range(12, 16):
            target[pl.ds(first_row + s, 1), :] = jnp.zeros((1, LANES), F32)

    def peer(p, carry):
        fill(fine, p * PEER_ROWS, p)
        return carry

    lax.fori_loop(0, 16, peer, 0)
    fill(lower, 0, 16)
    fill(upper, 0, 17)


def rest_density_kernel(
    lists, counts, live, table, ghosts, rho, first, energy, density, state, cols
):
    density[...] = rho[...]
    density[0:FIRST, :] = first[...]
    ghost_density(lists, counts, table, ghosts, density, cols, FIRST, live[0])
    thermal = energy[...]
    dens = density[...]
    state[0] = (2.0 / 3.0) * thermal / dens
    state[1] = jnp.sqrt((10.0 / 9.0) * thermal)
    state[2] = 4.0 * dens


def force_columns(cols, table, state, t):
    for i, f in enumerate((0, 1, 2, 4, 5, 6, 7)):
        cols[i] = columns(table[t, f : f + 1, :])
    for f in range(3):
        cols[7 + f] = columns(state[f, pl.ds(t, 1), :])


def force_one(cols, acc, source, sources_state, tile, row, first):
    xs, ys, zs, ms, us, vs, ws, hs = [spread(source[tile, f : f + 1, :]) for f in range(8)]
    ps, cs, rs = [spread(sources_state[f, pl.ds(row, 1), :]) for f in range(3)]
    for c in range(LANES // CHUNK):
        at = pl.ds(c * CHUNK, CHUNK)
        dx = cols[0, at, :] - xs
        dy = cols[1, at, :] - ys
        dz = cols[2, at, :] - zs
        r2 = dx * dx + dy * dy + dz * dz
        w = dx * (cols[3, at, :] - us) + dy * (cols[4, at, :] - vs) + dz * (cols[5, at, :] - ws)
        q = 1.0 / (cols[6, at, :] + hs)
        q2 = q * q
        u2 = r2 * q2
        u = u2 * lax.rsqrt(jnp.maximum(u2, TINY))
        tq = jnp.maximum(1.0 - u, 0.0) * q
        slope = (tq * tq) * (tq * q2)
        m = (jnp.maximum(w, 0.0) * q) / (u2 + 0.0025)
        visc = m * (cols[8, at, :] + cs + m) / (cols[9, at, :] + rs)
        coef = (slope * ms) * (cols[7, at, :] + ps + visc)
        terms = (coef * dx, coef * dy, coef * dz, coef * w)
        if first:
            for f in range(4):
                acc[f, at, :] = terms[f]
            acc[4, at, :] = m
        else:
            for f in range(4):
                acc[f, at, :] += terms[f]
            acc[4, at, :] = jnp.maximum(acc[4, at, :], m)


def force_totals(acc):
    scale = 210.0 / math.pi
    out = [scale * jnp.sum(acc[f].T, axis=0, keepdims=True) for f in range(3)]
    out.append(0.25 * scale * jnp.sum(acc[3].T, axis=0, keepdims=True))
    out.append(0.25 * jnp.max(acc[4].T, axis=0, keepdims=True))
    return out


def local_force_kernel(lists, counts, live, table, state, out, cols, acc):
    out[...] = jnp.zeros_like(out)

    def block(t, carry):
        force_columns(cols, table, state, t)
        force_one(cols, acc, table, state, t, t, True)

        def step(j, inner):
            s = lists[t * 8 + j]
            force_one(cols, acc, table, state, s, s, False)
            return inner

        lax.fori_loop(1, counts[t], step, 0)
        for f, row in enumerate(force_totals(acc)):
            out[f, pl.ds(t, 1), :] = row
        return carry

    lax.fori_loop(0, live[0], block, 0)


def ghost_force_kernel(
    lists, counts, live, table, state, ghosts, ghost_rho, smooth, local, out, least, ghost_state, cols, acc
):
    out[...] = local[...]
    for p in range(18):
        at = pl.ds(p * PEER_ROWS, PEER_ROWS)
        thermal = ghosts[p * PEER_TILES + 12 : p * PEER_TILES + 14].reshape(PEER_ROWS, LANES)
        dens = ghost_rho[at, :]
        ghost_state[0, at, :] = (2.0 / 3.0) * thermal / dens
        ghost_state[1, at, :] = jnp.sqrt((10.0 / 9.0) * thermal)
        ghost_state[2, at, :] = 4.0 * dens

    def block(t, carry):
        @pl.when(counts[t] > 0)
        def _():
            force_columns(cols, table, state, t)

            def one(j, is_first):
                g = lists[t * 8 + j]
                force_one(
                    cols, acc, ghosts, ghost_state, g - 2 * (g // PEER_ROWS), g, is_first
                )

            one(0, True)

            def step(j, inner):
                one(j, False)
                return inner

            lax.fori_loop(1, counts[t], step, 0)
            rows = force_totals(acc)
            at = pl.ds(t, 1)
            for f in range(4):
                out[f, at, :] += rows[f]
            out[4, at, :] = jnp.maximum(out[4, at, :], rows[4])

        return carry

    lax.fori_loop(0, live[0], block, 0)
    sound = state[1]
    step = COURANT * smooth[...] / (sound + 1.2 * (sound + 2.0 * out[4]))
    index = lax.broadcasted_iota(jnp.int32, step.shape, 0)
    least[0] = jnp.min(jnp.where(index < live[0], step, FAR_STEP))


def scale_kernel(least, forces, kick, heating):
    dt = least[0]

    def block(k, carry):
        row = pl.ds(k, 1)
        at = pl.ds(pl.multiple_of(k * LANES, LANES), LANES)
        for f in range(3):
            kick[f : f + 1, at] = dt * forces[f, row, :]
        return carry

    lax.fori_loop(0, forces.shape[1], block, 0)
    heating[...] = dt * forces[3]


def compacted(values, chosen):
    rank = jnp.sum(
        jnp.tril(jnp.ones((8, 8), jnp.int32), -1)[None] * chosen.astype(jnp.int32)[:, None, :], axis=2
    )
    hit = chosen[:, None, :] & (rank[:, None, :] == jnp.arange(8, dtype=jnp.int32)[None, :, None])
    lists = jnp.sum(jnp.where(hit, values[:, None, :], 0), axis=2)
    return lists.reshape(-1), jnp.sum(chosen.astype(jnp.int32), axis=1)


def shards(
    position, velocity, mass, smoothing, energy, live_blocks, send_list, nbr_list, nbr_count
):
    blocks = nbr_count.shape[0]
    mass2 = mass.reshape(blocks, LANES)
    smooth2 = smoothing.reshape(blocks, LANES)
    energy2 = energy.reshape(blocks, LANES)
    send = send_list.reshape(-1)

    table, fine, lower, upper = pl.pallas_call(
        pack_kernel,
        out_shape=(
            struct(blocks, 8, LANES),
            struct(16 * PEER_TILES, 8, LANES),
            struct(PEER_TILES, 8, LANES),
            struct(PEER_TILES, 8, LANES),
        ),
        in_specs=[SMEM] + [VMEM] * 5,
        out_specs=(VMEM,) * 4,
        name="pack",
    )(send, position, velocity, mass2, smooth2, energy2)

    def exchange(fine, lower, upper):
        shape = (16, fine.shape[0] // 16) + fine.shape[1:]
        arrived = lax.all_to_all(fine.reshape(shape), "gy", split_axis=0, concat_axis=0, tiled=True)
        size = lax.axis_size("gx")
        up = [(i, i + 1) for i in range(size - 1)]
        down = [(j, i) for i, j in up]
        before = lax.ppermute(upper, "gx", up)
        after = lax.ppermute(lower, "gx", down)
        return jnp.concatenate([arrived.reshape(fine.shape), before, after], axis=0)

    ghosts = exchange(fine, lower, upper)

    used = jnp.arange(8, dtype=jnp.int32)[None, :] < nbr_count[:, None]
    is_local = nbr_list < blocks
    local_lists, local_counts = compacted(nbr_list, used & is_local)
    slot = nbr_list - blocks
    ghost_lists, ghost_counts = compacted(slot + 4 * (slot // 12), used & ~is_local)

    cols4 = pltpu.VMEM((4, LANES, LANES), F32)
    local_rho = pl.pallas_call(
        local_density_kernel,
        out_shape=struct(blocks, LANES),
        in_specs=[SMEM] * 3 + [VMEM],
        out_specs=VMEM,
        scratch_shapes=[cols4],
        name="local_density",
    )(local_lists, local_counts, live_blocks, table)

    first, fine_rho, lower_rho, upper_rho = pl.pallas_call(
        first_density_kernel,
        out_shape=(
            struct(FIRST, LANES),
            struct(16 * PEER_ROWS, LANES),
            struct(PEER_ROWS, LANES),
            struct(PEER_ROWS, LANES),
        ),
        in_specs=[SMEM] * 3 + [VMEM] * 3,
        out_specs=(VMEM,) * 4,
        scratch_shapes=[cols4],
        name="first_density",
    )(send, ghost_lists, ghost_counts, table, ghosts, local_rho)

    ghost_rho = exchange(fine_rho, lower_rho, upper_rho)

    density, state = pl.pallas_call(
        rest_density_kernel,
        out_shape=(struct(blocks, LANES), struct(3, blocks, LANES)),
        in_specs=[SMEM] * 3 + [VMEM] * 5,
        out_specs=(VMEM,) * 2,
        scratch_shapes=[cols4],
        name="rest_density",
    )(ghost_lists, ghost_counts, live_blocks, table, ghosts, local_rho, first, energy2)

    cols10 = pltpu.VMEM((10, LANES, LANES), F32)
    acc5 = pltpu.VMEM((5, LANES, LANES), F32)
    local_force = pl.pallas_call(
        local_force_kernel,
        out_shape=struct(5, blocks, LANES),
        in_specs=[SMEM] * 3 + [VMEM] * 2,
        out_specs=VMEM,
        scratch_shapes=[cols10, acc5],
        name="local_force",
    )(local_lists, local_counts, live_blocks, table, state)

    forces, least = pl.pallas_call(
        ghost_force_kernel,
        out_shape=(struct(5, blocks, LANES), struct(1)),
        in_specs=[SMEM] * 3 + [VMEM] * 6,
        out_specs=(VMEM, SMEM),
        scratch_shapes=[pltpu.VMEM((3, 18 * PEER_ROWS, LANES), F32), cols10, acc5],
        name="ghost_force",
    )(
        ghost_lists,
        ghost_counts,
        live_blocks,
        table,
        state,
        ghosts,
        ghost_rho,
        smooth2,
        local_force,
    )

    timestep = lax.pmin(least, ("gx", "gy"))
    kick, heating = pl.pallas_call(
        scale_kernel,
        out_shape=(struct(3, blocks * LANES), struct(blocks, LANES)),
        in_specs=[SMEM, VMEM],
        out_specs=(VMEM,) * 2,
        name="scale",
    )(timestep, forces)
    return (density.reshape(-1), kick, heating.reshape(-1))


def solution(mesh):
    return jax.shard_map(
        shards,
        mesh=mesh,
        in_specs=(
            P(None, ("gx", "gy")),
            P(None, ("gx", "gy")),
            P(("gx", "gy")),
            P(("gx", "gy")),
            P(("gx", "gy")),
            P(("gx", "gy")),
            P(("gx", "gy"), None, None),
            P(("gx", "gy"), None),
            P(("gx", "gy")),
        ),
        out_specs=(P(("gx", "gy")), P(None, ("gx", "gy")), P(("gx", "gy"))),
        check_vma=False,
    )
```

time: 616 us -> 383 us (0.62); the launches traced: 611 us -> 386 us
  other arithmetic: 374 us -> 3.04 us
  Pallas kernels: 0 us -> 251 us
  local copies, waits for them, and re-layouts: 98.6 us -> 3.02 us
  waiting for transfers between devices: 18.6 us -> 0.02 us
  blocking collectives: 82.1 us -> 95.4 us
    reduce_sum x32 -> x4, other arithmetic: 298 us -> 1.25 us  [the longest x2 1.13 us: compacted(): return (lists.reshape(-1), jnp.sum(chosen.astype(jnp.int32), axis=1))]
    pallas_call x0 -> x7, Pallas kernels: none -> 251 us  [the longest x1 124 us: shards(): pl.pallas_call(local_force_kernel, out_shape=struct(5, blocks, LANES), in...]
    select_n x68 -> x1, other arithmetic: 48.1 us -> 0.07 us  [compacted(): jnp.tril(jnp.ones((8, 8), jnp.int32), -1)[None]]
    gather x52 -> x0, local copies, waits for them, and re-layouts: 34.7 us -> none  [the longest x16 10.5 us: density_group(): source_pos = wide_pos[:, chosen].reshape(3, group, list_width * block_size)]
    dynamic_slice x32 -> x0, local copies, waits for them, and re-layouts: 24.3 us -> none  [the longest x16 12.8 us: shards(): lax.map(force_group, (grouped_lists, usable_rows, grouped_rows))]
    slice x40 -> x0, local copies, waits for them, and re-layouts: 20.8 us -> none  [the longest x16 15 us: force_group(): weight = jnp.where(allowed, source_rows[6], 0.0)]
    dynamic_update_slice x48 -> x0, other arithmetic: 19.5 us -> none  [the longest x32 9.79 us: shards(): lax.map(density_group, (grouped_lists, usable_rows, grouped_pos, smooth.r...]
    all_to_all x2, waiting for transfers between devices: 18.6 us -> 0.01 us  [exchange(): lax.all_to_all(fine.reshape(shape), 'gy', split_axis=0, concat_axis=0, ti...]
  transfers between devices with their start and end apart: 6 -> 6, of which waited for: 2 -> 0; matrix products, arithmetic and copies ran while one was open for 2% -> 1% of each run, Pallas kernels for 0% -> 52%
where the time goes in v1:
time: 383 us; the launch traced here: 386 us
  Pallas kernels  251 us (66%)
  blocking collectives  95.4 us (25%)
  starting transfers between devices  32.6 us (9%)
    pallas_call x1, Pallas kernels, shards(): pl.pallas_call(local_force_kernel, out_shape=struct(5, blocks, LANES), in...  124 us
    pmin x1, blocking collectives, shards(): timestep = lax.pmin(least, ('gx', 'gy'))  95.4 us
    pallas_call x1, Pallas kernels, shards(): pl.pallas_call(local_density_kernel, out_shape=struct(blocks, LANES), in_...  69.2 us
    pallas_call x1, Pallas kernels, shards(): pl.pallas_call(ghost_force_kernel, out_shape=(struct(5, blocks, LANES), s...  29.7 us
    all_to_all x2, starting transfers between devices, exchange(): lax.all_to_all(fine.reshape(shape), 'gy', split_axis=0, concat_axis=0, ti...  16.1 us
    pallas_call x1, Pallas kernels, shards(): pl.pallas_call(first_density_kernel, out_shape=(struct(FIRST, LANES), str...  14.1 us
    ppermute x2, starting transfers between devices, exchange(): before = lax.ppermute(upper, 'gx', up)  13.9 us
  transfers between devices with their start and end apart: 6, of which 0 were waited for; matrix products, arithmetic and copies ran while one was open for 1% of the time, Pallas kernels for 52%

profile of v1, /device:TPU:1, one launch (start us, length us, event | category | flops | bytes accessed | tf_op | source)
XLA Modules:
  0.0 386.5 jit_solution(4516314016855775637)
XLA Ops:
  0.6 0.8 copy.26
  1.4 0.7 reshape.66.send
  2.1 3.6 pack.1
  5.7 12.6 %all-to-all-start = ((f32[16,14,8,128]{3,2,1,0:T(8,128)}), f32[16,14,8,128]{3,2,1,0:T(8,128)S(1)}, u32[]{:S(2)}, u32[]{:S(2)}) async-start(f32[16,14,8,128]{3,2,1,0:T(8,128)} %bitcast.10), calls=%async_computation | async-start | bytes 1835008 | tf_op jit(solution)/shard_map/all_to_all | solution.py:318
  18.2 0.0 copy-start.1
  18.2 1.3 collective-permute-start.1
  19.6 4.0 %collective-permute-start = (f32[14,8,128]{2,1,0:T(8,128)S(1)}, f32[14,8,128]{2,1,0:T(8,128)S(1)}, u32[]{:S(2)}, u32[]{:S(2)}) collective-permute-start(f32[14,8,128]{2,1,0:T(8,128)S(1)} %copy-done.2), channel_id=1, source_target_pairs={{0,16},{16,32},{32,48},{48,64},{64,80},{80,96},{96,112},{112,128},... | collective-permute-start | bytes 172040 | tf_op jit(solution)/shard_map/ppermute | solution.py:322
  23.6 0.5 convert_reduce_fusion
  24.1 0.6 convert_reduce_fusion.1
  24.7 0.1 fusion.6
  24.8 0.1 multiply_reduce_fusion
  24.9 0.1 copy.25
  25.0 0.7 reshape.65.lists
  26.3 0.1 copy.27
  26.4 0.7 reshape.72.lists
  27.1 69.2 %local_density.1.rho = f32[128,128]{1,0:T(8,128)} custom-call(s32[1024]{0:T(1024)} %reshape.72.lists, s32[128]{0:T(128)} %get-tuple-element.33.counts, s32[1]{0:T(128)S(6)} %copy.28.live, f32[128,8,128]{2,1,0:T(8,128)} %get-tuple-element.17.table), custom_call_target="tpu_custom_call" | custom-call | tf_op jit(solution)/shard_map/local_density/pallas_call | solution.py:335
  96.4 0.0 collective-permute-done.1
  96.4 0.0 collective-permute-done
  96.4 0.0 all-to-all-done
  96.4 1.0 pad_maximum_fusion.ghosts
  97.4 14.1 %first_density.1 = (f32[24,128]{1,0:T(8,128)}, f32[256,128]{1,0:T(8,128)}, f32[16,128]{1,0:T(8,128)}, f32[16,128]{1,0:T(8,128)}) custom-call(s32[216]{0:T(256)} %reshape.66.send, s32[1024]{0:T(1024)} %reshape.65.lists, s32[128]{0:T(128)} %get-tuple-element.36.counts, f32[128,8,128]{2,1,0:T(8,128)} %get-tuple-element.17.table, ...), custom_call_target="tpu_custom_call" | custom-call | tf_op jit(solution)/shard_map/first_density/pallas_call | solution.py:344
  111.5 3.6 all-to-all-start.1
  115.1 1.3 collective-permute-start.3
  116.4 9.9 %collective-permute-start.2 = (f32[16,128]{1,0:T(8,128)S(1)}, f32[16,128]{1,0:T(8,128)S(1)}, u32[]{:S(2)}, u32[]{:S(2)}) collective-permute-start(f32[16,128]{1,0:T(8,128)S(1)} %copy-done.4), channel_id=1, source_target_pairs={{0,16},{16,32},{32,48},{48,64},{64,80},{80,96},{96,112},{112,128},... | collective-permute-start | bytes 24584 | tf_op jit(solution)/shard_map/ppermute | solution.py:322
  126.3 7.3 %rest_density.1 = (f32[128,128]{1,0:T(8,128)}, f32[3,128,128]{2,1,0:T(8,128)}) custom-call(s32[1024]{0:T(1024)} %reshape.65.lists, s32[128]{0:T(128)} %get-tuple-element.36.counts, s32[1]{0:T(128)S(6)} %copy.28.live, f32[128,8,128]{2,1,0:T(8,128)} %get-tuple-element.17.table, f32[252,8,128]{2,1,0:T(8,128)} %pad_maximum_fusion.ghosts, ...), custom_call_target="tpu_custom_call" | custom-call | tf_op jit(solution)/shard_map/rest_density/pallas_call | solution.py:360
  133.7 123.9 %local_force.1.local = f32[5,128,128]{2,1,0:T(8,128)} custom-call(s32[1024]{0:T(1024)} %reshape.72.lists, s32[128]{0:T(128)} %get-tuple-element.33.counts, s32[1]{0:T(128)S(6)} %copy.28.live, f32[128,8,128]{2,1,0:T(8,128)} %get-tuple-element.17.table, f32[3,128,128]{2,1,0:T(8,128)} %get-tuple-element.23.state), custom_call_target="tpu_custom_call" | custom-call | tf_op jit(solution)/shard_map/local_force/pallas_call | solution.py:371
  257.6 0.0 collective-permute-done.2
  257.6 0.0 all-to-all-done.1
  257.6 0.7 pad_maximum_fusion.1.ghost_rho
  258.3 29.7 %ghost_force.1 = (f32[5,128,128]{2,1,0:T(8,128)}, f32[1]{0:T(128)}) custom-call(s32[1024]{0:T(1024)} %reshape.65.lists, s32[128]{0:T(128)} %get-tuple-element.36.counts, s32[1]{0:T(128)S(6)} %copy.28.live, f32[128,8,128]{2,1,0:T(8,128)} %get-tuple-element.17.table, f32[3,128,128]{2,1,0:T(8,128)} %get-tuple-element.23.state, ...), custom_call_target="tpu_custom_call" | custom-call | tf_op jit(solution)/shard_map/ghost_force/pallas_call | solution.py:380
  287.9 95.4 %pmin.7.least = f32[1]{0:T(128)} all-reduce(f32[1]{0:T(128)} %get-tuple-element.27), channel_id=1, replica_groups=mesh['gx'=16,'gy'=16] {'gx','gy'}, use_global_device_ids=true, to_apply=%region_6.7 | all-reduce | flops 1 | bytes 8 | tf_op jit(solution)/shard_map/pmin | solution.py:399
  383.4 3.1 scale.1
  (16 shorter events, 0.1 us)
Async XLA Ops:
  5.6 12.6 %copy-start.3 = (f32[14,8,128]{2,1,0:T(8,128)S(1)}, f32[14,8,128]{2,1,0:T(8,128)}, u32[]{:S(2)}) copy-start(f32[14,8,128]{2,1,0:T(8,128)} %get-tuple-element.20) | copy-start | bytes 172036
  5.6 13.9 %copy-start.2 = (f32[14,8,128]{2,1,0:T(8,128)S(1)}, f32[14,8,128]{2,1,0:T(8,128)}, u32[]{:S(2)}) copy-start(f32[14,8,128]{2,1,0:T(8,128)} %get-tuple-element.19) | copy-start | bytes 172036
  5.6 17.9 %copy-start = (s32[128,8]{0,1:T(8,128)S(1)}, s32[128,8]{0,1:T(8,128)}, u32[]{:S(2)}) copy-start(s32[128,8]{0,1:T(8,128)} %param.16) | copy-start | bytes 12292
  5.7 90.7 %all-to-all-start = ((f32[16,14,8,128]{3,2,1,0:T(8,128)}), f32[16,14,8,128]{3,2,1,0:T(8,128)S(1)}, u32[]{:S(2)}, u32[]{:S(2)}) async-start(f32[16,14,8,128]{3,2,1,0:T(8,128)} %bitcast.10), calls=%async_computation | async-start | bytes 1835008 | tf_op jit(solution)/shard_map/all_to_all | solution.py:318
  18.2 5.3 %copy-start.1 = (s32[128]{0:T(128)S(1)}, s32[128]{0:T(128)}, u32[]{:S(2)}) copy-start(s32[128]{0:T(128)} %param.17) | copy-start | bytes 1540
  18.2 78.1 %collective-permute-start.1 = (f32[14,8,128]{2,1,0:T(8,128)S(1)}, f32[14,8,128]{2,1,0:T(8,128)S(1)}, u32[]{:S(2)}, u32[]{:S(2)}) collective-permute-start(f32[14,8,128]{2,1,0:T(8,128)S(1)} %copy-done.3), channel_id=1, source_target_pairs={{16,0},{32,16},{48,32},{64,48},{80,64},{96,80},{112,96},{128,112},... | collective-permute-start | bytes 172040 | tf_op jit(solution)/shard_map/ppermute | solution.py:323
  19.6 76.8 %collective-permute-start = (f32[14,8,128]{2,1,0:T(8,128)S(1)}, f32[14,8,128]{2,1,0:T(8,128)S(1)}, u32[]{:S(2)}, u32[]{:S(2)}) collective-permute-start(f32[14,8,128]{2,1,0:T(8,128)S(1)} %copy-done.2), channel_id=1, source_target_pairs={{0,16},{16,32},{32,48},{48,64},{64,80},{80,96},{96,112},{112,128},... | collective-permute-start | bytes 172040 | tf_op jit(solution)/shard_map/ppermute | solution.py:322
  111.5 3.6 copy-start.5
  111.5 4.9 %copy-start.4 = (f32[16,128]{1,0:T(8,128)S(1)}, f32[16,128]{1,0:T(8,128)}, u32[]{:S(2)}) copy-start(f32[16,128]{1,0:T(8,128)} %get-tuple-element.25) | copy-start | bytes 24580
  111.5 146.1 %all-to-all-start.1 = ((f32[16,16,128]{2,1,0:T(8,128)}), f32[16,16,128]{2,1,0:T(8,128)S(1)}, u32[]{:S(2)}, u32[]{:S(2)}) async-start(f32[16,16,128]{2,1,0:T(8,128)} %bitcast.16), calls=%async_computation.1 | async-start | bytes 262144 | tf_op jit(solution)/shard_map/all_to_all | solution.py:318
  115.1 142.5 %collective-permute-start.3 = (f32[16,128]{1,0:T(8,128)S(1)}, f32[16,128]{1,0:T(8,128)S(1)}, u32[]{:S(2)}, u32[]{:S(2)}) collective-permute-start(f32[16,128]{1,0:T(8,128)S(1)} %copy-done.5), channel_id=1, source_target_pairs={{16,0},{32,16},{48,32},{64,48},{80,64},{96,80},{112,96},{128,112},... | collective-permute-start | bytes 24584 | tf_op jit(solution)/shard_map/ppermute | solution.py:323
  116.4 141.2 %collective-permute-start.2 = (f32[16,128]{1,0:T(8,128)S(1)}, f32[16,128]{1,0:T(8,128)S(1)}, u32[]{:S(2)}, u32[]{:S(2)}) collective-permute-start(f32[16,128]{1,0:T(8,128)S(1)} %copy-done.4), channel_id=1, source_target_pairs={{0,16},{16,32},{32,48},{48,64},{64,80},{80,96},{96,112},{112,128},... | collective-permute-start | bytes 24584 | tf_op jit(solution)/shard_map/ppermute | solution.py:322

commit v2 on v1

v2 whole, which is shorter than its diff:
```python
import math

import jax
import jax.numpy as jnp
from jax import lax
from jax.experimental import pallas as pl
from jax.experimental.pallas import tpu as pltpu
from jax.sharding import PartitionSpec as P

COURANT = 0.3
FAR_STEP = 1e30
TINY = 1e-30
LANES = 128
CHUNK = 8
FIRST = 24
PEER_TILES = 14
PEER_ROWS = 16
F32 = jnp.float32

SMEM = pl.BlockSpec(memory_space=pltpu.SMEM)
VMEM = pl.BlockSpec(memory_space=pltpu.VMEM)


def struct(*shape):
    return jax.ShapeDtypeStruct(shape, F32)


def columns(row):
    return jnp.broadcast_to(row, (LANES, LANES)).T


def spread(row):
    return jnp.broadcast_to(row, (CHUNK, LANES))


def pack_kernel(send, position, velocity, mass, smooth, energy, table, fine, lower, upper):
    blocks = mass.shape[0]

    def build(k, carry):
        at = pl.ds(pl.multiple_of(k * LANES, LANES), LANES)
        row = pl.ds(k, 1)
        table[k] = jnp.concatenate(
            [position[:, at], mass[row, :], -2.0 * velocity[:, at], smooth[row, :]], axis=0
        )
        return carry

    lax.fori_loop(0, blocks, build, 0)

    def fill(target, first_tile, p):
        for s in range(12):
            k = send[p * 12 + s]
            target[first_tile + s] = table[k]
            target[first_tile + 12 + s // 8, s % 8 : s % 8 + 1, :] = energy[pl.ds(k, 1), :]
        target[first_tile + 13, 4:8, :] = jnp.zeros((4, LANES), F32)

    def peer(p, carry):
        fill(fine, p * PEER_TILES, p)
        return carry

    lax.fori_loop(0, 16, peer, 0)
    fill(lower, 0, 16)
    fill(upper, 0, 17)


def over_blocks(order, lo, hi, prepare, gather, finish):
    @pl.when(hi > lo)
    def _():
        prepare(order[lo], 0)

        def pair(i, carry):
            for side in range(2):
                at = lo + 2 * i + side
                this = order[jnp.minimum(at, hi - 1)]
                after = order[jnp.minimum(at + 1, hi - 1)]
                before = order[jnp.minimum(jnp.maximum(at - 1, lo), hi - 1)]
                head, tail = gather(this, side)
                head()
                finish(before, 1 - side)
                prepare(after, 1 - side)
                tail()
            return carry

        lax.fori_loop(0, (hi - lo + 1) // 2, pair, 0)
        finish(order[hi - 1], 1)


def slots_of(lists, t, ghosts):
    def at(j):
        s = lists[j, t]
        if not ghosts:
            return s, s
        peer = (jnp.maximum(s - LANES, 0) * 171) >> 11
        return s + 2 * peer, s + 4 * peer

    return at


def head_and_tail(count, run):
    def head():
        run([0, 1, 2, 3], True)

    def tail():
        def two(i, carry):
            run([4 + 2 * i, 5 + 2 * i], False)
            return carry

        lax.fori_loop(0, (count - 4) // 2, two, 0)

        @pl.when(count % 2 == 1)
        def _():
            run([count - 1], False)

    return head, tail


def density_blocks(lists, counts, order, lo, hi, table, source, ghosts, out, cols, acc):
    def prepare(t, side):
        for f in range(3):
            cols[side][f] = columns(table[t, f : f + 1, :])
        h = table[t, 7:8, :]
        cols[side][3] = columns(0.25 / (h * h))

    def finish(t, side):
        h = table[t, 7:8, :]
        total = jnp.sum(acc[side][...].T, axis=0, keepdims=True)
        out[pl.ds(t, 1), :] = (21.0 / (4.0 * math.pi)) / (h * h * h) * total

    def gather(t, side):
        slot = slots_of(lists, t, ghosts)

        def run(js, first):
            tiles = [slot(j)[0] for j in js]
            rows = [[spread(source[k, f : f + 1, :]) for f in range(4)] for k in tiles]
            for c in range(LANES // CHUNK):
                at = pl.ds(c * CHUNK, CHUNK)
                xa, ya, za, scale = [cols[side][f, at, :] for f in range(4)]
                total = None if first else acc[side][at, :]
                for xs, ys, zs, ms in rows:
                    dx = xa - xs
                    dy = ya - ys
                    dz = za - zs
                    u2 = (dx * dx + dy * dy + dz * dz) * scale
                    u = u2 * lax.rsqrt(jnp.maximum(u2, TINY))
                    t1 = jnp.maximum(1.0 - u, 0.0)
                    t2 = t1 * t1
                    term = (t2 * ms) * (t2 * (1.25 - t1))
                    total = term if total is None else total + term
                acc[side][at, :] = total

        return head_and_tail(counts[t], run)

    over_blocks(order, lo, hi, prepare, gather, finish)


def pure_density_kernel(lists, counts, order, bounds, table, out, c0, c1, a0, a1):
    out[...] = jnp.zeros_like(out)
    density_blocks(
        lists, counts, order, 0, bounds[0], table, table, False, out, (c0, c1), (a0, a1)
    )


def first_density_kernel(
    send, lists, counts, order, bounds, table, source, rho, first, fine, lower, upper, c0, c1, a0, a1
):
    first[...] = rho[0:FIRST, :]
    density_blocks(
        lists, counts, order, bounds[0], bounds[1], table, source, True, first, (c0, c1), (a0, a1)
    )

    def fill(target, first_row, p):
        for s in range(12):
            target[pl.ds(first_row + s, 1), :] = first[pl.ds(send[p * 12 + s], 1), :]
        for s in range(12, 16):
            target[pl.ds(first_row + s, 1), :] = jnp.zeros((1, LANES), F32)

    def peer(p, carry):
        fill(fine, p * PEER_ROWS, p)
        return carry

    lax.fori_loop(0, 16, peer, 0)
    fill(lower, 0, 16)
    fill(upper, 0, 17)


def rest_density_kernel(
    lists, counts, order, bounds, table, source, rho, first, energy, density, state, c0, c1, a0, a1
):
    density[...] = rho[...]
    density[0:FIRST, :] = first[...]
    density_blocks(
        lists, counts, order, bounds[1], bounds[2], table, source, True, density, (c0, c1), (a0, a1)
    )
    thermal = energy[...]
    dens = density[...]
    state[0] = (2.0 / 3.0) * thermal / dens
    state[1] = jnp.sqrt((10.0 / 9.0) * thermal)
    state[2] = 4.0 * dens


def force_blocks(lists, counts, order, lo, hi, table, state, source, source_state, ghosts, out, cols, acc):
    def prepare(t, side):
        for i, f in enumerate((0, 1, 2, 4, 5, 6, 7)):
            cols[side][i] = columns(table[t, f : f + 1, :])
        for f in range(3):
            cols[side][7 + f] = columns(state[f, pl.ds(t, 1), :])

    def finish(t, side):
        at = pl.ds(t, 1)
        scale = 210.0 / math.pi
        for f in range(4):
            total = jnp.sum(acc[side][f].T, axis=0, keepdims=True)
            out[f, at, :] = (scale if f < 3 else 0.25 * scale) * total
        out[4, at, :] = 0.25 * jnp.max(acc[side][4].T, axis=0, keepdims=True)

    def gather(t, side):
        slot = slots_of(lists, t, ghosts)

        def run(js, first):
            slots = [slot(j) for j in js]
            for c in range(LANES // CHUNK):
                at = pl.ds(c * CHUNK, CHUNK)
                xa, ya, za, ua, va, wa, ha, pa, ca, ra = [cols[side][f, at, :] for f in range(10)]
                sums = None if first else [acc[side][f, at, :] for f in range(5)]
                for tile, row in slots:
                    xs, ys, zs, ms, us, vs, ws, hs = [
                        spread(source[tile, f : f + 1, :]) for f in range(8)
                    ]
                    ps, cs, rs = [spread(source_state[f, pl.ds(row, 1), :]) for f in range(3)]
                    dx = xa - xs
                    dy = ya - ys
                    dz = za - zs
                    r2 = dx * dx + dy * dy + dz * dz
                    w = dx * (ua - us) + dy * (va - vs) + dz * (wa - ws)
                    q = 1.0 / (ha + hs)
                    q2 = q * q
                    u2 = r2 * q2
                    u = u2 * lax.rsqrt(jnp.maximum(u2, TINY))
                    tq = jnp.maximum(1.0 - u, 0.0) * q
                    slope = (tq * tq) * (tq * q2)
                    m = (jnp.maximum(w, 0.0) * q) / (u2 + 0.0025)
                    visc = m * (ca + cs + m) / (ra + rs)
                    coef = (slope * ms) * (pa + ps + visc)
                    terms = [coef * dx, coef * dy, coef * dz, coef * w, m]
                    if sums is None:
                        sums = terms
                    else:
                        sums = [a + b for a, b in zip(sums[:4], terms[:4])] + [
                            jnp.maximum(sums[4], m)
                        ]
                for f in range(5):
                    acc[side][f, at, :] = sums[f]

        return head_and_tail(counts[t], run)

    over_blocks(order, lo, hi, prepare, gather, finish)


def pure_force_kernel(lists, counts, order, bounds, table, state, out, c0, c1, a0, a1):
    out[...] = jnp.zeros_like(out)
    force_blocks(
        lists, counts, order, 0, bounds[0], table, state, table, state, False, out, (c0, c1), (a0, a1)
    )


def mixed_force_kernel(
    lists, counts, order, bounds, table, state, source, ghost_rho, local, out, least, wide, c0, c1, a0, a1
):
    out[...] = local[...]
    blocks = table.shape[0]
    for f in range(3):
        wide[f, 0:blocks, :] = state[f]
    for p in range(18):
        at = pl.ds(blocks + p * PEER_ROWS, PEER_ROWS)
        tile = blocks + p * PEER_TILES + 12
        thermal = source[tile : tile + 2].reshape(PEER_ROWS, LANES)
        dens = ghost_rho[p * PEER_ROWS : (p + 1) * PEER_ROWS, :]
        wide[0, at, :] = (2.0 / 3.0) * thermal / dens
        wide[1, at, :] = jnp.sqrt((10.0 / 9.0) * thermal)
        wide[2, at, :] = 4.0 * dens
    force_blocks(
        lists, counts, order, bounds[0], bounds[2], table, state, source, wide, True, out, (c0, c1), (a0, a1)
    )
    sound = state[1]
    smooth = table[:, 7:8, :].reshape(blocks, LANES)
    step = COURANT * smooth / (sound + 1.2 * (sound + 2.0 * out[4]))
    index = lax.broadcasted_iota(jnp.int32, step.shape, 0)
    smallest = jnp.min(jnp.where(index < bounds[3], step, FAR_STEP))
    least[...] = jnp.full(least.shape, smallest, F32)


def scale_kernel(least, forces, kick, heating):
    dt = jnp.min(least[...])

    def block(k, carry):
        row = pl.ds(k, 1)
        at = pl.ds(pl.multiple_of(k * LANES, LANES), LANES)
        for f in range(3):
            kick[f : f + 1, at] = dt * forces[f, row, :]
        return carry

    lax.fori_loop(0, forces.shape[1], block, 0)
    heating[...] = dt * forces[3]


def block_order(nbr_list, nbr_count, live):
    blocks, width = nbr_list.shape
    k = jnp.arange(blocks, dtype=jnp.int32)
    used = jnp.arange(width, dtype=jnp.int32)[None, :] < nbr_count[:, None]
    mixed = jnp.any(used & (nbr_list >= blocks), axis=1)
    kind = jnp.where(mixed, jnp.where(k < FIRST, 1, 2), 0)
    kind = jnp.where(k < live, kind, 3)
    key = kind * blocks + k
    rank = jnp.sum((key[None, :] < key[:, None]).astype(jnp.int32), axis=1)
    order = jnp.sum(jnp.where(rank[None, :] == k[:, None], k[None, :], 0), axis=1)
    bounds = jnp.sum((kind[None, :] <= jnp.arange(3, dtype=jnp.int32)[:, None]).astype(jnp.int32), axis=1)
    return order, jnp.concatenate([bounds, live])


def shards(
    position, velocity, mass, smoothing, energy, live_blocks, send_list, nbr_list, nbr_count
):
    blocks = nbr_count.shape[0]
    mass2 = mass.reshape(blocks, LANES)
    smooth2 = smoothing.reshape(blocks, LANES)
    energy2 = energy.reshape(blocks, LANES)
    send = send_list.reshape(-1)

    table, fine, lower, upper = pl.pallas_call(
        pack_kernel,
        out_shape=(
            struct(blocks, 8, LANES),
            struct(16 * PEER_TILES, 8, LANES),
            struct(PEER_TILES, 8, LANES),
            struct(PEER_TILES, 8, LANES),
        ),
        in_specs=[SMEM] + [VMEM] * 5,
        out_specs=(VMEM,) * 4,
        name="pack",
    )(send, position, velocity, mass2, smooth2, energy2)

    def exchange(fine, lower, upper):
        shape = (16, fine.shape[0] // 16) + fine.shape[1:]
        arrived = lax.all_to_all(fine.reshape(shape), "gy", split_axis=0, concat_axis=0, tiled=True)
        size = lax.axis_size("gx")
        up = [(i, i + 1) for i in range(size - 1)]
        down = [(j, i) for i, j in up]
        before = lax.ppermute(upper, "gx", up)
        after = lax.ppermute(lower, "gx", down)
        return jnp.concatenate([arrived.reshape(fine.shape), before, after], axis=0)

    ghosts = exchange(fine, lower, upper)
    source = jnp.concatenate([table, ghosts], axis=0)
    lists = nbr_list.T
    order, bounds = block_order(nbr_list, nbr_count, live_blocks)

    small = [pltpu.VMEM((4, LANES, LANES), F32)] * 2 + [pltpu.VMEM((LANES, LANES), F32)] * 2
    large = [pltpu.VMEM((10, LANES, LANES), F32)] * 2 + [pltpu.VMEM((5, LANES, LANES), F32)] * 2
    pure_rho = pl.pallas_call(
        pure_density_kernel,
        out_shape=struct(blocks, LANES),
        in_specs=[SMEM] * 4 + [VMEM],
        out_specs=VMEM,
        scratch_shapes=small,
        name="pure_density",
    )(lists, nbr_count, order, bounds, table)

    first, fine_rho, lower_rho, upper_rho = pl.pallas_call(
        first_density_kernel,
        out_shape=(
            struct(FIRST, LANES),
            struct(16 * PEER_ROWS, LANES),
            struct(PEER_ROWS, LANES),
            struct(PEER_ROWS, LANES),
        ),
        in_specs=[SMEM] * 5 + [VMEM] * 3,
        out_specs=(VMEM,) * 4,
        scratch_shapes=small,
        name="first_density",
    )(send, lists, nbr_count, order, bounds, table, source, pure_rho)

    ghost_rho = exchange(fine_rho, lower_rho, upper_rho)

    density, state = pl.pallas_call(
        rest_density_kernel,
        out_shape=(struct(blocks, LANES), struct(3, blocks, LANES)),
        in_specs=[SMEM] * 4 + [VMEM] * 5,
        out_specs=(VMEM,) * 2,
        scratch_shapes=small,
        name="rest_density",
    )(lists, nbr_count, order, bounds, table, source, pure_rho, first, energy2)

    pure_force = pl.pallas_call(
        pure_force_kernel,
        out_shape=struct(5, blocks, LANES),
        in_specs=[SMEM] * 4 + [VMEM] * 2,
        out_specs=VMEM,
        scratch_shapes=large,
        name="pure_force",
    )(lists, nbr_count, order, bounds, table, state)

    devices = lax.axis_size("gx") * lax.axis_size("gy")
    forces, least = pl.pallas_call(
        mixed_force_kernel,
        out_shape=(struct(5, blocks, LANES), struct(devices, LANES)),
        in_specs=[SMEM] * 4 + [VMEM] * 5,
        out_specs=(VMEM,) * 2,
        scratch_shapes=[pltpu.VMEM((3, blocks + 18 * PEER_ROWS, LANES), F32)] + large,
        name="mixed_force",
    )(lists, nbr_count, order, bounds, table, state, source, ghost_rho, pure_force)

    steps = lax.all_to_all(
        least.reshape(devices, 1, LANES), ("gx", "gy"), split_axis=0, concat_axis=0, tiled=True
    )
    kick, heating = pl.pallas_call(
        scale_kernel,
        out_shape=(struct(3, blocks * LANES), struct(blocks, LANES)),
        in_specs=[VMEM] * 2,
        out_specs=(VMEM,) * 2,
        name="scale",
    )(steps.reshape(devices, LANES), forces)
    return (density.reshape(-1), kick, heating.reshape(-1))


def solution(mesh):
    return jax.shard_map(
        shards,
        mesh=mesh,
        in_specs=(
            P(None, ("gx", "gy")),
            P(None, ("gx", "gy")),
            P(("gx", "gy")),
            P(("gx", "gy")),
            P(("gx", "gy")),
            P(("gx", "gy")),
            P(("gx", "gy"), None, None),
            P(("gx", "gy"), None),
            P(("gx", "gy")),
        ),
        out_specs=(P(("gx", "gy")), P(None, ("gx", "gy")), P(("gx", "gy"))),
        check_vma=False,
    )
```

time: 383 us -> 259 us (0.68); the launches traced: 386 us -> 257 us
  Pallas kernels: 251 us -> 143 us
  blocking collectives: 95.4 us -> 60.5 us
  starting transfers between devices: 32.6 us -> 47.1 us
    pallas_call x3, Pallas kernels: 223 us -> 116 us  [the longest x1 51.1 us: shards(): pl.pallas_call(pure_force_kernel, out_shape=struct(5, blocks, LANES), in_...]
    pmin x1 -> x0, blocking collectives: 95.4 us -> none  [shards(): timestep = lax.pmin(least, ('gx', 'gy'))]
    all_to_all x0 -> x1, blocking collectives: none -> 60.5 us  [shards(): lax.all_to_all(least.reshape(devices, 1, LANES), ('gx', 'gy'), split_axis...]
    all_to_all x2, starting transfers between devices: 16.1 us -> 33.6 us  [exchange(): lax.all_to_all(fine.reshape(shape), 'gy', split_axis=0, concat_axis=0, ti...]
  transfers between devices with their start and end apart: 6 -> 6, of which waited for: 0 -> 0; matrix products, arithmetic and copies ran while one was open for 1% -> 1% of each run, Pallas kernels for 52% -> 32%
where the time goes in v2:
time: 259 us; the launch traced here: 257 us
  Pallas kernels  143 us (55%)
  blocking collectives  60.5 us (23%)
  starting transfers between devices  47.1 us (18%)
  other arithmetic  3.43 us (1%)
    all_to_all x1, blocking collectives, shards(): lax.all_to_all(least.reshape(devices, 1, LANES), ('gx', 'gy'), split_axis...  60.5 us
    pallas_call x1, Pallas kernels, shards(): pl.pallas_call(pure_force_kernel, out_shape=struct(5, blocks, LANES), in_...  51.1 us
    pallas_call x1, Pallas kernels, shards(): pl.pallas_call(mixed_force_kernel, out_shape=(struct(5, blocks, LANES), s...  43.5 us
    all_to_all x2, starting transfers between devices, exchange(): lax.all_to_all(fine.reshape(shape), 'gy', split_axis=0, concat_axis=0, ti...  33.6 us
    pallas_call x1, Pallas kernels, shards(): pl.pallas_call(pure_density_kernel, out_shape=struct(blocks, LANES), in_s...  21.1 us
    pallas_call x1, Pallas kernels, shards(): pl.pallas_call(first_density_kernel, out_shape=(struct(FIRST, LANES), str...  12 us
    ppermute x2, starting transfers between devices, exchange(): before = lax.ppermute(upper, 'gx', up)  11 us
    pallas_call x1, Pallas kernels, shards(): pl.pallas_call(rest_density_kernel, out_shape=(struct(blocks, LANES), str...  9.12 us
  transfers between devices with their start and end apart: 6, of which 0 were waited for; matrix products, arithmetic and copies ran while one was open for 1% of the time, Pallas kernels for 32%

profile of v2, /device:TPU:1, one launch (start us, length us, event | category | flops | bytes accessed | tf_op | source)
XLA Modules:
  0.0 257.0 jit_solution(12919316002487668523)
XLA Ops:
  0.6 0.0 copy-start.2
  0.6 0.0 copy-start.1
  0.7 0.8 copy.15
  1.4 0.7 reshape.76.send
  2.1 3.6 %pack.1 = (f32[128,8,128]{2,1,0:T(8,128)}, f32[224,8,128]{2,1,0:T(8,128)}, f32[14,8,128]{2,1,0:T(8,128)}, f32[14,8,128]{2,1,0:T(8,128)}) custom-call(s32[216]{0:T(256)} %reshape.76.send, f32[3,16384]{1,0:T(4,128)} %position.1, f32[3,16384]{1,0:T(4,128)} %velocity.1, f32[128,128]{1,0:T(8,128)} %bitcast.29, f32[128,128]{1,0:T(8,128)} %bitcast.30, ...), custom_call_target="tpu_custom_call" | custom-call | tf_op jit(solution)/shard_map/pack/pallas_call | solution.py:328
  5.7 0.0 copy-start
  5.7 12.6 %all-to-all-start = ((f32[16,14,8,128]{3,2,1,0:T(8,128)}), f32[16,14,8,128]{3,2,1,0:T(8,128)S(1)}, u32[]{:S(2)}, u32[]{:S(2)}) async-start(f32[16,14,8,128]{3,2,1,0:T(8,128)} %bitcast.17), calls=%async_computation | async-start | bytes 1835008 | tf_op jit(solution)/shard_map/all_to_all | solution.py:343
  18.3 3.2 %collective-permute-start = (f32[14,8,128]{2,1,0:T(8,128)S(1)}, f32[14,8,128]{2,1,0:T(8,128)S(1)}, u32[]{:S(2)}, u32[]{:S(2)}) collective-permute-start(f32[14,8,128]{2,1,0:T(8,128)S(1)} %copy-done.4), channel_id=1, source_target_pairs={{0,16},{16,32},{32,48},{48,64},{64,80},{80,96},{96,112},{112,128},... | collective-permute-start | bytes 172040 | tf_op jit(solution)/shard_map/ppermute | solution.py:347
  21.5 1.3 collective-permute-start.1
  23.5 0.1 convert_reduce_fusion.1
  23.6 0.2 convert_reduce_fusion
  23.8 0.6 select_reduce_fusion.order
  24.4 0.6 pad_add_fusion.bounds
  25.0 21.1 %pure_density.1.rho = f32[128,128]{1,0:T(8,128)} custom-call(s32[8,128]{1,0:T(8,128)} %bitcast.22, s32[128]{0:T(128)} %counts.9, s32[128]{0:T(128)} %select_reduce_fusion.order, s32[4]{0:T(128)} %pad_add_fusion.bounds, f32[128,8,128]{2,1,0:T(8,128)} %get-tuple-element.17.table), custom_call_target="tpu_custom_call" | custom-call | tf_op jit(solution)/shard_map/pure_density/pallas_call | solution.py:358
  46.1 0.0 collective-permute-done
  46.1 0.0 collective-permute-done.1
  46.1 0.0 all-to-all-done
  46.1 0.0 copy-done
  46.1 1.2 pad_maximum_fusion.source
  47.3 12.0 %first_density.1 = (f32[24,128]{1,0:T(8,128)}, f32[256,128]{1,0:T(8,128)}, f32[16,128]{1,0:T(8,128)}, f32[16,128]{1,0:T(8,128)}) custom-call(s32[216]{0:T(256)} %reshape.76.send, s32[8,128]{1,0:T(8,128)} %bitcast.23, s32[128]{0:T(128)} %counts.9, s32[128]{0:T(128)} %select_reduce_fusion.order, s32[4]{0:T(128)} %pad_add_fusion.bounds, ...), custom_call_target="tpu_custom_call" | custom-call | tf_op jit(solution)/shard_map/first_density/pallas_call | solution.py:367
  59.4 21.0 %all-to-all-start.1 = ((f32[16,16,128]{2,1,0:T(8,128)}), f32[16,16,128]{2,1,0:T(8,128)S(1)}, u32[]{:S(2)}, u32[]{:S(2)}) async-start(f32[16,16,128]{2,1,0:T(8,128)} %bitcast.27), calls=%async_computation.1 | async-start | bytes 262144 | tf_op jit(solution)/shard_map/all_to_all | solution.py:343
  80.4 7.8 %collective-permute-start.2 = (f32[16,128]{1,0:T(8,128)}, f32[16,128]{1,0:T(8,128)S(1)}, u32[]{:S(2)}, u32[]{:S(2)}) collective-permute-start(f32[16,128]{1,0:T(8,128)} %get-tuple-element.25), channel_id=1, source_target_pairs={{0,16},{16,32},{32,48},{48,64},{64,80},{80,96},{96,112},{112,128},... | collective-permute-start | bytes 24584 | tf_op jit(solution)/shard_map/ppermute | solution.py:347
  88.2 1.3 collective-permute-start.3
  89.5 9.1 %rest_density.1 = (f32[128,128]{1,0:T(8,128)}, f32[3,128,128]{2,1,0:T(8,128)}) custom-call(s32[8,128]{1,0:T(8,128)} %bitcast.24, s32[128]{0:T(128)} %counts.9, s32[128]{0:T(128)} %select_reduce_fusion.order, s32[4]{0:T(128)} %pad_add_fusion.bounds, f32[128,8,128]{2,1,0:T(8,128)} %get-tuple-element.17.table, f32[380,8,128]{2,1,0:T(8,128)} %pad_maximum_fusion.source, ...), custom_call_target="tpu_custom_call" | custom-call | tf_op jit(solution)/shard_map/rest_density/pallas_call | solution.py:383
  98.6 51.1 %pure_force.1.local = f32[5,128,128]{2,1,0:T(8,128)} custom-call(s32[8,128]{1,0:T(8,128)} %bitcast.25, s32[128]{0:T(128)} %counts.9, s32[128]{0:T(128)} %select_reduce_fusion.order, s32[4]{0:T(128)} %pad_add_fusion.bounds, f32[128,8,128]{2,1,0:T(8,128)} %get-tuple-element.17.table, f32[3,128,128]{2,1,0:T(8,128)} %get-tuple-element.23.state), custom_call_target="tpu_custom_call" | custom-call | tf_op jit(solution)/shard_map/pure_force/pallas_call | solution.py:392
  149.7 0.0 collective-permute-done.2
  149.7 0.0 collective-permute-done.3
  149.7 0.0 all-to-all-done.1
  149.7 0.7 pad_maximum_fusion.1.ghost_rho
  150.3 43.5 %mixed_force.1 = (f32[5,128,128]{2,1,0:T(8,128)}, f32[256,128]{1,0:T(8,128)}) custom-call(s32[8,128]{1,0:T(8,128)} %bitcast.26, s32[128]{0:T(128)} %counts.9, s32[128]{0:T(128)} %select_reduce_fusion.order, s32[4]{0:T(128)} %pad_add_fusion.bounds, f32[128,8,128]{2,1,0:T(8,128)} %get-tuple-element.17.table, f32[3,128,128]{2,1,0:T(8,128)} %get-tuple-element.23.state, ...), custom_call_target="tpu_custom_call" | custom-call | tf_op jit(solution)/shard_map/mixed_force/pallas_call | solution.py:402
  193.8 60.5 %all_to_all.15 = f32[256,1,128]{2,1,0:T(1,128)} all-to-all(f32[256,1,128]{2,1,0:T(1,128)} %bitcast.28), channel_id=1, replica_groups=mesh['gx'=16,'gy'=16] {'gx','gy'}, dimensions={0} | all-to-all | bytes 262144 | tf_op jit(solution)/shard_map/all_to_all | solution.py:411
  254.3 2.7 %scale.1 = (f32[3,16384]{1,0:T(4,128)}, f32[128,128]{1,0:T(8,128)}) custom-call(f32[256,128]{1,0:T(8,128)} %bitcast.18, f32[5,128,128]{2,1,0:T(8,128)} %get-tuple-element.28.forces), custom_call_target="tpu_custom_call" | custom-call | tf_op jit(solution)/shard_map/scale/pallas_call | solution.py:414
  (8 shorter events, 0.0 us)
Async XLA Ops:
  0.6 22.8 %copy-start.2 = (s32[128]{0:T(128)S(1)}, s32[128]{0:T(128)}, u32[]{:S(2)}) copy-start(s32[128]{0:T(128)} %counts.9) | copy-start | bytes 1540
  0.6 22.8 %copy-start.1 = (s32[128,8]{0,1:T(8,128)S(1)}, s32[128,8]{0,1:T(8,128)}, u32[]{:S(2)}) copy-start(s32[128,8]{0,1:T(8,128)} %param.16) | copy-start | bytes 12292
  5.7 12.6 %copy-start.4 = (f32[14,8,128]{2,1,0:T(8,128)S(1)}, f32[14,8,128]{2,1,0:T(8,128)}, u32[]{:S(2)}) copy-start(f32[14,8,128]{2,1,0:T(8,128)} %get-tuple-element.19) | copy-start | bytes 172036
  5.7 15.8 %copy-start.3 = (f32[14,8,128]{2,1,0:T(8,128)S(1)}, f32[14,8,128]{2,1,0:T(8,128)}, u32[]{:S(2)}) copy-start(f32[14,8,128]{2,1,0:T(8,128)} %get-tuple-element.20) | copy-start | bytes 172036
  5.7 40.4 %copy-start = (f32[128,8,128]{2,1,0:T(8,128)S(1)}, f32[128,8,128]{2,1,0:T(8,128)}, u32[]{:S(2)}) copy-start(f32[128,8,128]{2,1,0:T(8,128)} %get-tuple-element.17.table) | copy-start | bytes 1572868
  5.7 40.4 %all-to-all-start = ((f32[16,14,8,128]{3,2,1,0:T(8,128)}), f32[16,14,8,128]{3,2,1,0:T(8,128)S(1)}, u32[]{:S(2)}, u32[]{:S(2)}) async-start(f32[16,14,8,128]{3,2,1,0:T(8,128)} %bitcast.17), calls=%async_computation | async-start | bytes 1835008 | tf_op jit(solution)/shard_map/all_to_all | solution.py:343
  18.3 27.8 %collective-permute-start = (f32[14,8,128]{2,1,0:T(8,128)S(1)}, f32[14,8,128]{2,1,0:T(8,128)S(1)}, u32[]{:S(2)}, u32[]{:S(2)}) collective-permute-start(f32[14,8,128]{2,1,0:T(8,128)S(1)} %copy-done.4), channel_id=1, source_target_pairs={{0,16},{16,32},{32,48},{48,64},{64,80},{80,96},{96,112},{112,128},... | collective-permute-start | bytes 172040 | tf_op jit(solution)/shard_map/ppermute | solution.py:347
  21.5 24.6 %collective-permute-start.1 = (f32[14,8,128]{2,1,0:T(8,128)S(1)}, f32[14,8,128]{2,1,0:T(8,128)S(1)}, u32[]{:S(2)}, u32[]{:S(2)}) collective-permute-start(f32[14,8,128]{2,1,0:T(8,128)S(1)} %copy-done.3), channel_id=1, source_target_pairs={{16,0},{32,16},{48,32},{64,48},{80,64},{96,80},{112,96},{128,112},... | collective-permute-start | bytes 172040 | tf_op jit(solution)/shard_map/ppermute | solution.py:348
  59.4 90.3 %all-to-all-start.1 = ((f32[16,16,128]{2,1,0:T(8,128)}), f32[16,16,128]{2,1,0:T(8,128)S(1)}, u32[]{:S(2)}, u32[]{:S(2)}) async-start(f32[16,16,128]{2,1,0:T(8,128)} %bitcast.27), calls=%async_computation.1 | async-start | bytes 262144 | tf_op jit(solution)/shard_map/all_to_all | solution.py:343
  80.4 69.3 %collective-permute-start.2 = (f32[16,128]{1,0:T(8,128)}, f32[16,128]{1,0:T(8,128)S(1)}, u32[]{:S(2)}, u32[]{:S(2)}) collective-permute-start(f32[16,128]{1,0:T(8,128)} %get-tuple-element.25), channel_id=1, source_target_pairs={{0,16},{16,32},{32,48},{48,64},{64,80},{80,96},{96,112},{112,128},... | collective-permute-start | bytes 24584 | tf_op jit(solution)/shard_map/ppermute | solution.py:347
  88.2 61.5 %collective-permute-start.3 = (f32[16,128]{1,0:T(8,128)}, f32[16,128]{1,0:T(8,128)S(1)}, u32[]{:S(2)}, u32[]{:S(2)}) collective-permute-start(f32[16,128]{1,0:T(8,128)} %get-tuple-element.26), channel_id=1, source_target_pairs={{16,0},{32,16},{48,32},{64,48},{80,64},{96,80},{112,96},{128,112},... | collective-permute-start | bytes 24584 | tf_op jit(solution)/shard_map/ppermute | solution.py:348

commit v3 on v2

--- a/solution.py
+++ b/solution.py
@@ -1,3 +1,4 @@
+import functools
 import math
 
 import jax
@@ -33,7 +34,30 @@
     return jnp.broadcast_to(row, (CHUNK, LANES))
 
 
-def pack_kernel(send, position, velocity, mass, smooth, energy, table, fine, lower, upper):
+def block_order(lists, counts, live):
+    width, blocks = lists.shape
+    k = lax.broadcasted_iota(jnp.int32, (1, blocks), 1)
+    used = lax.broadcasted_iota(jnp.int32, lists.shape, 0) < counts
+    mixed = jnp.max(jnp.where(used & (lists >= blocks), 1.0, 0.0), axis=0, keepdims=True) > 0.0
+    kind = jnp.where(mixed, jnp.where(k < FIRST, 1, 2), 0)
+    kind = jnp.where(k < live, kind, 3)
+    key = (kind * blocks + k).astype(F32)
+    key_column = jnp.broadcast_to(key, (blocks, blocks)).T
+    rank = jnp.sum(jnp.where(key_column < key, 1.0, 0.0), axis=0, keepdims=True)
+    rank_column = jnp.broadcast_to(rank, (blocks, blocks)).T
+    sublane = lax.broadcasted_iota(jnp.int32, (blocks, blocks), 0).astype(F32)
+    hit = rank_column == k.astype(F32)
+    order = jnp.sum(jnp.where(hit, sublane, 0.0), axis=0, keepdims=True).astype(jnp.int32)
+    ends = jnp.full((1, blocks), live, jnp.int32)
+    for c in range(3):
+        end = jnp.sum(jnp.where(kind <= c, 1.0, 0.0), axis=1, keepdims=True).astype(jnp.int32)
+        ends = jnp.where(k == c, end, ends)
+    return order, ends
+
+
+def pack_kernel(
+    send, live, lists, counts, position, velocity, mass, smooth, energy, table, fine, lower, upper, order, bounds
+):
     blocks = mass.shape[0]
 
     def build(k, carry):
@@ -48,7 +72,7 @@
 
     def fill(target, first_tile, p):
         for s in range(12):
-            k = send[p * 12 + s]
+            k = send[s, 0, p]
             target[first_tile + s] = table[k]
             target[first_tile + 12 + s // 8, s % 8 : s % 8 + 1, :] = energy[pl.ds(k, 1), :]
         target[first_tile + 13, 4:8, :] = jnp.zeros((4, LANES), F32)
@@ -60,28 +84,38 @@
     lax.fori_loop(0, 16, peer, 0)
     fill(lower, 0, 16)
     fill(upper, 0, 17)
+    order[...], bounds[...] = block_order(lists[...], counts[...], live[0])
 
 
 def over_blocks(order, lo, hi, prepare, gather, finish):
     @pl.when(hi > lo)
     def _():
-        prepare(order[lo], 0)
+        for step in prepare(order[lo], 0):
+            step()
+
+        def one(at, side):
+            this = order[at]
+            after = order[jnp.minimum(at + 1, hi - 1)]
+            before = order[jnp.maximum(at - 1, lo)]
+            gather(this, side, finish(before, 1 - side), prepare(after, 1 - side))
 
         def pair(i, carry):
-            for side in range(2):
-                at = lo + 2 * i + side
-                this = order[jnp.minimum(at, hi - 1)]
-                after = order[jnp.minimum(at + 1, hi - 1)]
-                before = order[jnp.minimum(jnp.maximum(at - 1, lo), hi - 1)]
-                head, tail = gather(this, side)
-                head()
-                finish(before, 1 - side)
-                prepare(after, 1 - side)
-                tail()
+            at = lo + 2 * i
+            one(at, 0)
+
+            @pl.when(at + 1 < hi)
+            def _():
+                one(at + 1, 1)
+
             return carry
 
         lax.fori_loop(0, (hi - lo + 1) // 2, pair, 0)
-        finish(order[hi - 1], 1)
+        for side in range(2):
+
+            @pl.when((hi - lo - 1) % 2 == side)
+            def _():
+                for step in finish(order[hi - 1], side):
+                    step()
 
 
 def slots_of(lists, t, ghosts):
@@ -95,40 +129,50 @@
     return at
 
 
-def head_and_tail(count, run):
-    def head():
-        run([0, 1, 2, 3], True)
-
-    def tail():
-        def two(i, carry):
-            run([4 + 2 * i, 5 + 2 * i], False)
-            return carry
-
-        lax.fori_loop(0, (count - 4) // 2, two, 0)
-
-        @pl.when(count % 2 == 1)
-        def _():
-            run([count - 1], False)
-
-    return head, tail
+def gather_all(count, run, folds, makes):
+    run([0, 1], True, folds)
+
+    @pl.when(count > 3)
+    def _():
+        run([2, 3], False, makes)
+
+    def two(i, carry):
+        run([4 + 2 * i, 5 + 2 * i], False, [])
+        return carry
+
+    lax.fori_loop(0, (count - 4) // 2, two, 0)
+
+    @pl.when(count % 2 == 1)
+    def _():
+        run([count - 1], False, [])
+
+
+def between(steps, c):
+    chunks = LANES // CHUNK
+    for step in steps[c * len(steps) // chunks : (c + 1) * len(steps) // chunks]:
+        step()
 
 
 def density_blocks(lists, counts, order, lo, hi, table, source, ghosts, out, cols, acc):
     def prepare(t, side):
-        for f in range(3):
-            cols[side][f] = columns(table[t, f : f + 1, :])
-        h = table[t, 7:8, :]
-        cols[side][3] = columns(0.25 / (h * h))
+        def make(f):
+            h = table[t, 7:8, :]
+            cols[side][f] = columns(table[t, f : f + 1, :] if f < 3 else 0.25 / (h * h))
+
+        return [functools.partial(make, f) for f in range(4)]
 
     def finish(t, side):
-        h = table[t, 7:8, :]
-        total = jnp.sum(acc[side][...].T, axis=0, keepdims=True)
-        out[pl.ds(t, 1), :] = (21.0 / (4.0 * math.pi)) / (h * h * h) * total
-
-    def gather(t, side):
+        def fold():
+            h = table[t, 7:8, :]
+            total = jnp.sum(acc[side][...].T, axis=0, keepdims=True)
+            out[pl.ds(t, 1), :] = (21.0 / (4.0 * math.pi)) / (h * h * h) * total
+
+        return [fold]
+
+    def gather(t, side, folds, makes):
         slot = slots_of(lists, t, ghosts)
 
-        def run(js, first):
+        def run(js, first, steps):
             tiles = [slot(j)[0] for j in js]
             rows = [[spread(source[k, f : f + 1, :]) for f in range(4)] for k in tiles]
             for c in range(LANES // CHUNK):
@@ -146,8 +190,9 @@
                     term = (t2 * ms) * (t2 * (1.25 - t1))
                     total = term if total is None else total + term
                 acc[side][at, :] = total
-
-        return head_and_tail(counts[t], run)
+                between(steps, c)
+
+        gather_all(counts[t], run, folds, makes)
 
     over_blocks(order, lo, hi, prepare, gather, finish)
 
@@ -169,7 +214,7 @@
 
     def fill(target, first_row, p):
         for s in range(12):
-            target[pl.ds(first_row + s, 1), :] = first[pl.ds(send[p * 12 + s], 1), :]
+            target[pl.ds(first_row + s, 1), :] = first[pl.ds(send[s, 0, p], 1), :]
         for s in range(12, 16):
             target[pl.ds(first_row + s, 1), :] = jnp.zeros((1, LANES), F32)
 
@@ -197,25 +242,36 @@
     state[2] = 4.0 * dens
 
 
-def force_blocks(lists, counts, order, lo, hi, table, state, source, source_state, ghosts, out, cols, acc):
+def force_blocks(lists, counts, order, lo, hi, table, state, source, source_state, ghosts, out, rest, cols, acc):
     def prepare(t, side):
-        for i, f in enumerate((0, 1, 2, 4, 5, 6, 7)):
-            cols[side][i] = columns(table[t, f : f + 1, :])
-        for f in range(3):
-            cols[side][7 + f] = columns(state[f, pl.ds(t, 1), :])
+        def make(i):
+            if i < 7:
+                f = (0, 1, 2, 4, 5, 6, 7)[i]
+                cols[side][i] = columns(table[t, f : f + 1, :])
+            else:
+                cols[side][i] = columns(state[i - 7, pl.ds(t, 1), :])
+
+        return [functools.partial(make, i) for i in range(10)]
 
     def finish(t, side):
         at = pl.ds(t, 1)
         scale = 210.0 / math.pi
-        for f in range(4):
-            total = jnp.sum(acc[side][f].T, axis=0, keepdims=True)
-            out[f, at, :] = (scale if f < 3 else 0.25 * scale) * total
-        out[4, at, :] = 0.25 * jnp.max(acc[side][4].T, axis=0, keepdims=True)
-
-    def gather(t, side):
+
+        def fold(f):
+            if f < 3:
+                lanes = pl.ds(pl.multiple_of(t * LANES, LANES), LANES)
+                out[f : f + 1, lanes] = scale * jnp.sum(acc[side][f].T, axis=0, keepdims=True)
+            elif f == 3:
+                rest[0, at, :] = 0.25 * scale * jnp.sum(acc[side][3].T, axis=0, keepdims=True)
+            else:
+                rest[1, at, :] = 0.25 * jnp.max(acc[side][4].T, axis=0, keepdims=True)
+
+        return [functools.partial(fold, f) for f in range(5)]
+
+    def gather(t, side, folds, makes):
         slot = slots_of(lists, t, ghosts)
 
-        def run(js, first):
+        def run(js, first, steps):
             slots = [slot(j) for j in js]
             for c in range(LANES // CHUNK):
                 at = pl.ds(c * CHUNK, CHUNK)
@@ -249,23 +305,28 @@
                         ]
                 for f in range(5):
                     acc[side][f, at, :] = sums[f]
-
-        return head_and_tail(counts[t], run)
+                between(steps, c)
+
+        gather_all(counts[t], run, folds, makes)
 
     over_blocks(order, lo, hi, prepare, gather, finish)
 
 
-def pure_force_kernel(lists, counts, order, bounds, table, state, out, c0, c1, a0, a1):
+def pure_force_kernel(lists, counts, order, bounds, table, state, out, rest, c0, c1, a0, a1):
     out[...] = jnp.zeros_like(out)
+    rest[...] = jnp.zeros_like(rest)
     force_blocks(
-        lists, counts, order, 0, bounds[0], table, state, table, state, False, out, (c0, c1), (a0, a1)
+        lists, counts, order, 0, bounds[0], table, state, table, state, False, out, rest,
+        (c0, c1), (a0, a1)
     )
 
 
 def mixed_force_kernel(
-    lists, counts, order, bounds, table, state, source, ghost_rho, local, out, least, wide, c0, c1, a0, a1
+    lists, counts, order, bounds, table, state, source, rho, rho_before, rho_after,
+    local, local_rest, out, rest, least, wide, c0, c1, a0, a1
 ):
     out[...] = local[...]
+    rest[...] = local_rest[...]
     blocks = table.shape[0]
     for f in range(3):
         wide[f, 0:blocks, :] = state[f]
@@ -273,47 +334,29 @@
         at = pl.ds(blocks + p * PEER_ROWS, PEER_ROWS)
         tile = blocks + p * PEER_TILES + 12
         thermal = source[tile : tile + 2].reshape(PEER_ROWS, LANES)
-        dens = ghost_rho[p * PEER_ROWS : (p + 1) * PEER_ROWS, :]
+        if p < 16:
+            dens = rho[p * PEER_ROWS : (p + 1) * PEER_ROWS, :]
+        else:
+            dens = (rho_before if p == 16 else rho_after)[...]
         wide[0, at, :] = (2.0 / 3.0) * thermal / dens
         wide[1, at, :] = jnp.sqrt((10.0 / 9.0) * thermal)
         wide[2, at, :] = 4.0 * dens
     force_blocks(
-        lists, counts, order, bounds[0], bounds[2], table, state, source, wide, True, out, (c0, c1), (a0, a1)
+        lists, counts, order, bounds[0], bounds[2], table, state, source, wide, True, out, rest,
+        (c0, c1), (a0, a1)
     )
     sound = state[1]
     smooth = table[:, 7:8, :].reshape(blocks, LANES)
-    step = COURANT * smooth / (sound + 1.2 * (sound + 2.0 * out[4]))
+    step = COURANT * smooth / (sound + 1.2 * (sound + 2.0 * rest[1]))
     index = lax.broadcasted_iota(jnp.int32, step.shape, 0)
     smallest = jnp.min(jnp.where(index < bounds[3], step, FAR_STEP))
     least[...] = jnp.full(least.shape, smallest, F32)
 
 
-def scale_kernel(least, forces, kick, heating):
+def scale_kernel(least, forces, rest, kick, heating):
     dt = jnp.min(least[...])
-
-    def block(k, carry):
-        row = pl.ds(k, 1)
-        at = pl.ds(pl.multiple_of(k * LANES, LANES), LANES)
-        for f in range(3):
-            kick[f : f + 1, at] = dt * forces[f, row, :]
-        return carry
-
-    lax.fori_loop(0, forces.shape[1], block, 0)
-    heating[...] = dt * forces[3]
-
-
-def block_order(nbr_list, nbr_count, live):
-    blocks, width = nbr_list.shape
-    k = jnp.arange(blocks, dtype=jnp.int32)
-    used = jnp.arange(width, dtype=jnp.int32)[None, :] < nbr_count[:, None]
-    mixed = jnp.any(used & (nbr_list >= blocks), axis=1)
-    kind = jnp.where(mixed, jnp.where(k < FIRST, 1, 2), 0)
-    kind = jnp.where(k < live, kind, 3)
-    key = kind * blocks + k
-    rank = jnp.sum((key[None, :] < key[:, None]).astype(jnp.int32), axis=1)
-    order = jnp.sum(jnp.where(rank[None, :] == k[:, None], k[None, :], 0), axis=1)
-    bounds = jnp.sum((kind[None, :] <= jnp.arange(3, dtype=jnp.int32)[:, None]).astype(jnp.int32), axis=1)
-    return order, jnp.concatenate([bounds, live])
+    kick[...] = dt * forces[...]
+    heating[...] = dt * rest[0]
 
 
 def shards(
@@ -323,20 +366,35 @@
     mass2 = mass.reshape(blocks, LANES)
     smooth2 = smoothing.reshape(blocks, LANES)
     energy2 = energy.reshape(blocks, LANES)
-    send = send_list.reshape(-1)
-
-    table, fine, lower, upper = pl.pallas_call(
+    send = jnp.transpose(send_list, (2, 0, 1))
+    lists = nbr_list.T
+
+    table, fine, lower, upper, order, bounds = pl.pallas_call(
         pack_kernel,
         out_shape=(
             struct(blocks, 8, LANES),
             struct(16 * PEER_TILES, 8, LANES),
             struct(PEER_TILES, 8, LANES),
             struct(PEER_TILES, 8, LANES),
+            jax.ShapeDtypeStruct((1, blocks), jnp.int32),
+            jax.ShapeDtypeStruct((1, blocks), jnp.int32),
         ),
-        in_specs=[SMEM] + [VMEM] * 5,
-        out_specs=(VMEM,) * 4,
+        in_specs=[SMEM] * 2 + [VMEM] * 7,
+        out_specs=(VMEM,) * 6,
         name="pack",
-    )(send, position, velocity, mass2, smooth2, energy2)
+    )(
+        send,
+        live_blocks,
+        lists,
+        nbr_count.reshape(1, blocks),
+        position,
+        velocity,
+        mass2,
+        smooth2,
+        energy2,
+    )
+    order = order.reshape(-1)
+    bounds = bounds.reshape(-1)
 
     def exchange(fine, lower, upper):
         shape = (16, fine.shape[0] // 16) + fine.shape[1:]
@@ -346,12 +404,10 @@
         down = [(j, i) for i, j in up]
         before = lax.ppermute(upper, "gx", up)
         after = lax.ppermute(lower, "gx", down)
-        return jnp.concatenate([arrived.reshape(fine.shape), before, after], axis=0)
+        return arrived.reshape(fine.shape), before, after
 
     ghosts = exchange(fine, lower, upper)
-    source = jnp.concatenate([table, ghosts], axis=0)
-    lists = nbr_list.T
-    order, bounds = block_order(nbr_list, nbr_count, live_blocks)
+    source = jnp.concatenate([table, *ghosts], axis=0)
 
     small = [pltpu.VMEM((4, LANES, LANES), F32)] * 2 + [pltpu.VMEM((LANES, LANES), F32)] * 2
     large = [pltpu.VMEM((10, LANES, LANES), F32)] * 2 + [pltpu.VMEM((5, LANES, LANES), F32)] * 2
@@ -391,22 +447,22 @@
 
     pure_force = pl.pallas_call(
         pure_force_kernel,
-        out_shape=struct(5, blocks, LANES),
+        out_shape=(struct(3, blocks * LANES), struct(2, blocks, LANES)),
         in_specs=[SMEM] * 4 + [VMEM] * 2,
-        out_specs=VMEM,
+        out_specs=(VMEM,) * 2,
         scratch_shapes=large,
         name="pure_force",
     )(lists, nbr_count, order, bounds, table, state)
 
     devices = lax.axis_size("gx") * lax.axis_size("gy")
-    forces, least = pl.pallas_call(
+    forces, rest, least = pl.pallas_call(
         mixed_force_kernel,
-        out_shape=(struct(5, blocks, LANES), struct(devices, LANES)),
-        in_specs=[SMEM] * 4 + [VMEM] * 5,
-        out_specs=(VMEM,) * 2,
+        out_shape=(struct(3, blocks * LANES), struct(2, blocks, LANES), struct(devices, LANES)),
+        in_specs=[SMEM] * 4 + [VMEM] * 8,
+        out_specs=(VMEM,) * 3,
         scratch_shapes=[pltpu.VMEM((3, blocks + 18 * PEER_ROWS, LANES), F32)] + large,
         name="mixed_force",
-    )(lists, nbr_count, order, bounds, table, state, source, ghost_rho, pure_force)
+    )(lists, nbr_count, order, bounds, table, state, source, *ghost_rho, *pure_force)
 
     steps = lax.all_to_all(
         least.reshape(devices, 1, LANES), ("gx", "gy"), split_axis=0, concat_axis=0, tiled=True
@@ -414,10 +470,10 @@
     kick, heating = pl.pallas_call(
         scale_kernel,
         out_shape=(struct(3, blocks * LANES), struct(blocks, LANES)),
-        in_specs=[VMEM] * 2,
+        in_specs=[VMEM] * 3,
         out_specs=(VMEM,) * 2,
         name="scale",
-    )(steps.reshape(devices, LANES), forces)
+    )(steps.reshape(devices, LANES), forces, rest)
     return (density.reshape(-1), kick, heating.reshape(-1))
 
 

time: 259 us -> 253 us (0.977)
  Pallas kernels: 143 us -> 184 us
  blocking collectives: 60.5 us -> 27.1 us
  starting transfers between devices: 47.1 us -> 33.9 us
    all_to_all x1, blocking collectives: 60.5 us -> 27.1 us  [shards(): lax.all_to_all(least.reshape(devices, 1, LANES), ('gx', 'gy'), split_axis...]
    pallas_call x2, Pallas kernels: 94.5 us -> 127 us  [the longest x1 78.8 us: shards(): pl.pallas_call(pure_force_kernel, out_shape=(struct(3, blocks * LANES), s...]
    all_to_all x2, starting transfers between devices: 33.6 us -> 18 us  [exchange(): lax.all_to_all(fine.reshape(shape), 'gy', split_axis=0, concat_axis=0, ti...]
    pallas_call x1, Pallas kernels: 21.1 us -> 30.1 us  [shards(): pl.pallas_call(pure_density_kernel, out_shape=struct(blocks, LANES), in_s...]
  transfers between devices with their start and end apart: 6 -> 6, of which waited for: 0 -> 0; matrix products, arithmetic and copies ran while one was open for 1% -> 0% of each run, Pallas kernels for 32% -> 48%
where the time goes in v3:
time: 253 us; the launch traced here: 249 us
  Pallas kernels  184 us (73%)
  starting transfers between devices  33.9 us (13%)
  blocking collectives  27.1 us (11%)
    pallas_call x1, Pallas kernels, shards(): pl.pallas_call(pure_force_kernel, out_shape=(struct(3, blocks * LANES), s...  78.8 us
    pallas_call x1, Pallas kernels, shards(): pl.pallas_call(mixed_force_kernel, out_shape=(struct(3, blocks * LANES),...  47.8 us
    pallas_call x1, Pallas kernels, shards(): pl.pallas_call(pure_density_kernel, out_shape=struct(blocks, LANES), in_s...  30.1 us
    all_to_all x1, blocking collectives, shards(): lax.all_to_all(least.reshape(devices, 1, LANES), ('gx', 'gy'), split_axis...  27.1 us
    all_to_all x2, starting transfers between devices, exchange(): lax.all_to_all(fine.reshape(shape), 'gy', split_axis=0, concat_axis=0, ti...  18 us
    ppermute x2, starting transfers between devices, exchange(): before = lax.ppermute(upper, 'gx', up)  13.3 us
    pallas_call x1, Pallas kernels, shards(): pl.pallas_call(first_density_kernel, out_shape=(struct(FIRST, LANES), str...  11 us
    pallas_call x1, Pallas kernels, shards(): pl.pallas_call(rest_density_kernel, out_shape=(struct(blocks, LANES), str...  10.9 us
  transfers between devices with their start and end apart: 6, of which 0 were waited for; matrix products, arithmetic and copies ran while one was open for 0% of the time, Pallas kernels for 48%

profile of v3, /device:TPU:1, one launch (start us, length us, event | category | flops | bytes accessed | tf_op | source)
XLA Modules:
  0.0 248.6 jit_solution(9272780640081920686)
XLA Ops:
  1.3 3.6 %pack.1 = (f32[128,8,128]{2,1,0:T(8,128)}, f32[224,8,128]{2,1,0:T(8,128)}, f32[14,8,128]{2,1,0:T(8,128)}, f32[14,8,128]{2,1,0:T(8,128)}, s32[1,128]{1,0:T(1,128)}, /*index=5*/s32[1,128]{1,0:T(1,128)}) custom-call(s32[12,1,18]{2,1,0:T(1,128)} %bitcast.34, s32[1]{0:T(128)S(6)} %copy.13.live, s32[8,128]{1,0:T(8,128)} %bitcast.24, s32[1,128]{1,0:T(1,128)} %bitcast.36, ...), custom_call_target="tpu_custom_call" | custom-call | tf_op jit(solution)/shard_map/pack/pallas_call | solution.py:372
  4.9 0.0 copy-start.5
  4.9 0.0 copy-start.4
  4.9 0.0 copy-start
  5.0 12.6 %all-to-all-start = ((f32[16,14,8,128]{3,2,1,0:T(8,128)}), f32[16,14,8,128]{3,2,1,0:T(8,128)S(1)}, u32[]{:S(2)}, u32[]{:S(2)}) async-start(f32[16,14,8,128]{3,2,1,0:T(8,128)} %bitcast.19), calls=%async_computation | async-start | bytes 1835008 | tf_op jit(solution)/shard_map/all_to_all | solution.py:401
  17.5 0.0 copy-done.5
  17.5 3.2 %collective-permute-start = (f32[14,8,128]{2,1,0:T(8,128)S(1)}, f32[14,8,128]{2,1,0:T(8,128)S(1)}, u32[]{:S(2)}, u32[]{:S(2)}) collective-permute-start(f32[14,8,128]{2,1,0:T(8,128)S(1)} %copy-done.5), channel_id=1, source_target_pairs={{0,16},{16,32},{32,48},{48,64},{64,80},{80,96},{96,112},{112,128},... | collective-permute-start | bytes 172040 | tf_op jit(solution)/shard_map/ppermute | solution.py:405
  20.7 0.0 copy-done.4
  20.8 1.3 collective-permute-start.1
  22.1 30.1 %pure_density.1.rho = f32[128,128]{1,0:T(8,128)} custom-call(s32[8,128]{1,0:T(8,128)} %bitcast.25, s32[128]{0:T(128)} %counts.9, s32[128]{0:T(128)} %bitcast.37, s32[128]{0:T(128)} %bitcast.42, f32[128,8,128]{2,1,0:T(8,128)} %get-tuple-element.24.table), custom_call_target="tpu_custom_call" | custom-call | tf_op jit(solution)/shard_map/pure_density/pallas_call | solution.py:414
  52.2 0.0 collective-permute-done
  52.2 0.0 collective-permute-done.1
  52.2 0.0 all-to-all-done
  52.2 0.0 copy-done
  52.2 1.3 pad_maximum_fusion.source
  53.4 11.0 %first_density.1 = (f32[24,128]{1,0:T(8,128)}, f32[256,128]{1,0:T(8,128)}, f32[16,128]{1,0:T(8,128)}, f32[16,128]{1,0:T(8,128)}) custom-call(s32[12,1,18]{2,1,0:T(1,128)} %bitcast.35, s32[8,128]{1,0:T(8,128)} %bitcast.26, s32[128]{0:T(128)} %counts.9, s32[128]{0:T(128)} %bitcast.38, s32[128]{0:T(128)} %bitcast.43, f32[128,8,128]{2,1,0:T(8,128)} %get-tuple-element.24.table, ...), custom_call_target="tpu_custom_call" | custom-call | tf_op jit(solution)/shard_map/first_density/pallas_call | solution.py:423
  64.5 5.5 %all-to-all-start.1 = ((f32[16,16,128]{2,1,0:T(8,128)}), f32[16,16,128]{2,1,0:T(8,128)S(1)}, u32[]{:S(2)}, u32[]{:S(2)}) async-start(f32[16,16,128]{2,1,0:T(8,128)} %bitcast.30), calls=%async_computation.1 | async-start | bytes 262144 | tf_op jit(solution)/shard_map/all_to_all | solution.py:401
  69.9 10.1 %collective-permute-start.2 = (f32[16,128]{1,0:T(8,128)}, f32[16,128]{1,0:T(8,128)S(1)}, u32[]{:S(2)}, u32[]{:S(2)}) collective-permute-start(f32[16,128]{1,0:T(8,128)} %get-tuple-element.32), channel_id=1, source_target_pairs={{0,16},{16,32},{32,48},{48,64},{64,80},{80,96},{96,112},{112,128},... | collective-permute-start | bytes 24584 | tf_op jit(solution)/shard_map/ppermute | solution.py:405
  80.1 1.3 collective-permute-start.3
  81.4 10.9 %rest_density.1 = (f32[128,128]{1,0:T(8,128)}, f32[3,128,128]{2,1,0:T(8,128)}) custom-call(s32[8,128]{1,0:T(8,128)} %bitcast.27, s32[128]{0:T(128)} %counts.9, s32[128]{0:T(128)} %bitcast.39, s32[128]{0:T(128)} %bitcast.44, f32[128,8,128]{2,1,0:T(8,128)} %get-tuple-element.24.table, f32[380,8,128]{2,1,0:T(8,128)} %pad_maximum_fusion.source, ...), custom_call_target="tpu_custom_call" | custom-call | tf_op jit(solution)/shard_map/rest_density/pallas_call | solution.py:439
  92.3 78.8 %pure_force.1 = (f32[3,16384]{1,0:T(4,128)}, f32[2,128,128]{2,1,0:T(8,128)}) custom-call(s32[8,128]{1,0:T(8,128)} %bitcast.28, s32[128]{0:T(128)} %counts.9, s32[128]{0:T(128)} %bitcast.40, s32[128]{0:T(128)} %bitcast.45, f32[128,8,128]{2,1,0:T(8,128)} %get-tuple-element.24.table, f32[3,128,128]{2,1,0:T(8,128)} %get-tuple-element.30.state), custom_call_target="tpu_custom_call" | custom-call | tf_op jit(solution)/shard_map/pure_force/pallas_call | solution.py:448
  171.1 0.0 collective-permute-done.2.rho_before
  171.1 0.0 collective-permute-done.3.rho_after
  171.1 0.0 copy-start.3
  171.1 0.0 all-to-all-done.1
  171.1 0.0 copy-start.1
  171.1 0.6 copy-done.2
  171.7 0.0 copy-done.3
  171.7 0.1 copy-done.1
  171.8 47.8 %mixed_force.1 = (f32[3,16384]{1,0:T(4,128)}, f32[2,128,128]{2,1,0:T(8,128)}, f32[256,128]{1,0:T(8,128)}) custom-call(s32[8,128]{1,0:T(8,128)} %bitcast.29, s32[128]{0:T(128)} %counts.9, s32[128]{0:T(128)} %bitcast.41, s32[128]{0:T(128)} %bitcast.46, f32[128,8,128]{2,1,0:T(8,128)} %get-tuple-element.24.table, f32[3,128,128]{2,1,0:T(8,128)} %get-tuple-element.30.state, ...), custom_call_target="tpu_custom_call" | custom-call | tf_op jit(solution)/shard_map/mixed_force/pallas_call | solution.py:458
  219.5 27.1 %all_to_all.15 = f32[256,1,128]{2,1,0:T(1,128)} all-to-all(f32[256,1,128]{2,1,0:T(1,128)} %bitcast.31), channel_id=1, replica_groups=mesh['gx'=16,'gy'=16] {'gx','gy'}, dimensions={0} | all-to-all | bytes 262144 | tf_op jit(solution)/shard_map/all_to_all | solution.py:467
  246.6 1.9 scale.1
  (1 shorter events, 0.0 us)
Async XLA Ops:
  4.9 12.6 %copy-start.5 = (f32[14,8,128]{2,1,0:T(8,128)S(1)}, f32[14,8,128]{2,1,0:T(8,128)}, u32[]{:S(2)}) copy-start(f32[14,8,128]{2,1,0:T(8,128)} %get-tuple-element.26) | copy-start | bytes 172036
  4.9 15.8 %copy-start.4 = (f32[14,8,128]{2,1,0:T(8,128)S(1)}, f32[14,8,128]{2,1,0:T(8,128)}, u32[]{:S(2)}) copy-start(f32[14,8,128]{2,1,0:T(8,128)} %get-tuple-element.27) | copy-start | bytes 172036
  4.9 47.2 %copy-start = (f32[128,8,128]{2,1,0:T(8,128)S(1)}, f32[128,8,128]{2,1,0:T(8,128)}, u32[]{:S(2)}) copy-start(f32[128,8,128]{2,1,0:T(8,128)} %get-tuple-element.24.table) | copy-start | bytes 1572868
  5.0 47.2 %all-to-all-start = ((f32[16,14,8,128]{3,2,1,0:T(8,128)}), f32[16,14,8,128]{3,2,1,0:T(8,128)S(1)}, u32[]{:S(2)}, u32[]{:S(2)}) async-start(f32[16,14,8,128]{3,2,1,0:T(8,128)} %bitcast.19), calls=%async_computation | async-start | bytes 1835008 | tf_op jit(solution)/shard_map/all_to_all | solution.py:401
  17.5 34.6 %collective-permute-start = (f32[14,8,128]{2,1,0:T(8,128)S(1)}, f32[14,8,128]{2,1,0:T(8,128)S(1)}, u32[]{:S(2)}, u32[]{:S(2)}) collective-permute-start(f32[14,8,128]{2,1,0:T(8,128)S(1)} %copy-done.5), channel_id=1, source_target_pairs={{0,16},{16,32},{32,48},{48,64},{64,80},{80,96},{96,112},{112,128},... | collective-permute-start | bytes 172040 | tf_op jit(solution)/shard_map/ppermute | solution.py:405
  20.8 31.4 %collective-permute-start.1 = (f32[14,8,128]{2,1,0:T(8,128)S(1)}, f32[14,8,128]{2,1,0:T(8,128)S(1)}, u32[]{:S(2)}, u32[]{:S(2)}) collective-permute-start(f32[14,8,128]{2,1,0:T(8,128)S(1)} %copy-done.4), channel_id=1, source_target_pairs={{16,0},{32,16},{48,32},{64,48},{80,64},{96,80},{112,96},{128,112},... | collective-permute-start | bytes 172040 | tf_op jit(solution)/shard_map/ppermute | solution.py:406
  64.5 106.6 %all-to-all-start.1 = ((f32[16,16,128]{2,1,0:T(8,128)}), f32[16,16,128]{2,1,0:T(8,128)S(1)}, u32[]{:S(2)}, u32[]{:S(2)}) async-start(f32[16,16,128]{2,1,0:T(8,128)} %bitcast.30), calls=%async_computation.1 | async-start | bytes 262144 | tf_op jit(solution)/shard_map/all_to_all | solution.py:401
  69.9 101.2 %collective-permute-start.2 = (f32[16,128]{1,0:T(8,128)}, f32[16,128]{1,0:T(8,128)S(1)}, u32[]{:S(2)}, u32[]{:S(2)}) collective-permute-start(f32[16,128]{1,0:T(8,128)} %get-tuple-element.32), channel_id=1, source_target_pairs={{0,16},{16,32},{32,48},{48,64},{64,80},{80,96},{96,112},{112,128},... | collective-permute-start | bytes 24584 | tf_op jit(solution)/shard_map/ppermute | solution.py:405
  80.1 91.0 %collective-permute-start.3 = (f32[16,128]{1,0:T(8,128)}, f32[16,128]{1,0:T(8,128)S(1)}, u32[]{:S(2)}, u32[]{:S(2)}) collective-permute-start(f32[16,128]{1,0:T(8,128)} %get-tuple-element.33), channel_id=1, source_target_pairs={{16,0},{32,16},{48,32},{64,48},{80,64},{96,80},{112,96},{128,112},... | collective-permute-start | bytes 24584 | tf_op jit(solution)/shard_map/ppermute | solution.py:406
  171.1 0.6 copy-start.2
  171.1 0.6 copy-start.3
  171.1 0.6 copy-start.1
